TPU v7x, 32 devices: a whole 2x2x4 slice. The times are simulated.
32 devices in a mesh: grp: 4 (over z), dev: 8 (over y, x, core).
Axes of the slice: x: 2, y: 2, z: 4, core: 2. Of those that a mesh axis runs over, the one named last changes fastest.
Arguments:
- atoms: bfloat16 [8192, 768], P(('grp', 'dev')), may hold values from -6 to 6
- positions: float32 [3, 8192], P(None, ('grp', 'dev')), may hold values from -6 to 6
- segment: int32 [8192], P(('grp', 'dev')), may hold values from 0 to 8191, as said below
- item_time: float32 [8192], P(('grp', 'dev')), may hold values from 0 to 1, as said below
- time_weight: bfloat16 [128, 768], P(None, ('grp', 'dev')), may hold values from -0.5 to 0.5
- norm1_gain: bfloat16 [768], P(('grp', 'dev')), may hold values from 0.5 to 1.5
- norm1_bias: bfloat16 [768], P(('grp', 'dev')), may hold values from -3 to 3
- qkv_weight: bfloat16 [768, 2304], P(('grp', 'dev')), may hold values from -0.21875 to 0.21875
- out_weight: bfloat16 [768, 768], P(('grp', 'dev')), may hold values from -1.75 to 1.75
- norm2_gain: bfloat16 [768], P(('grp', 'dev')), may hold values from 0.5 to 1.5
- norm2_bias: bfloat16 [768], P(('grp', 'dev')), may hold values from -3 to 3
- ffn_in: bfloat16 [768, 3072], P(('grp', 'dev')), may hold values from -0.21875 to 0.21875
- ffn_in_bias: bfloat16 [3072], P(('grp', 'dev')), may hold values from -3 to 3
- ffn_out: bfloat16 [3072, 768], P(('grp', 'dev')), may hold values from -0.109375 to 0.109375
- ffn_out_bias: bfloat16 [768], P(('grp', 'dev')), may hold values from -3 to 3
- pair_weight: bfloat16 [128, 32], replicated, may hold values from -4 to 4
- kernel_mean: float32 [128], replicated, may hold values from 0 to 12
- kernel_width: float32 [128], replicated, may hold values from 0.5 to 3
- cotangent: bfloat16 [8192, 768], P(('grp', 'dev')), may hold values from -6 to 6
Outputs:
- output: bfloat16 [8192, 768], P(('grp', 'dev'))
- grad_atoms: float32 [8192, 768], P(('grp', 'dev'))
- grad_time_weight: float32 [128, 768], P(None, ('grp', 'dev'))
- grad_norm1_gain: float32 [768], P(('grp', 'dev'))
- grad_norm1_bias: float32 [768], P(('grp', 'dev'))
- grad_qkv_weight: float32 [768, 2304], P(('grp', 'dev'))
- grad_out_weight: float32 [768, 768], P(('grp', 'dev'))
- grad_norm2_gain: float32 [768], P(('grp', 'dev'))
- grad_norm2_bias: float32 [768], P(('grp', 'dev'))
- grad_ffn_in: float32 [768, 3072], P(('grp', 'dev'))
- grad_ffn_in_bias: float32 [3072], P(('grp', 'dev'))
- grad_ffn_out: float32 [3072, 768], P(('grp', 'dev'))
- grad_ffn_out_bias: float32 [768], P(('grp', 'dev'))
- grad_pair_weight: float32 [128, 32], replicated
- grad_kernel_mean: float32 [128], replicated
- grad_kernel_width: float32 [128], replicated
Inputs may be any that keep to these rules, and one draw needn't show every extreme that they name: `segment`: an atom's item number is the index of the last atom of its item; numbers never fall along the atoms; each item is a run of equal numbers inside one aligned block of 1024 atoms and holds 1 to 1024 atoms; in every draw some block is one item of 1024 atoms. `item_time`: equal for all atoms of one item.
All inputs are finite; a program needn't handle non-finite values.
Results may differ from a plain program's by a relative error of at most 0.012.
The roundings to bfloat16 on the way count: a program that leaves them out, or rounds other values in their place, can miss the bound.
Values may be sent and summed in bfloat16 or wider, within the bound.
A program may use at most 256 MiB of HBM per device.

v0:
```python
from functools import partial
import math

import jax
import jax.numpy as jnp
from jax import lax
from jax.sharding import PartitionSpec as P

D = 768
HEADS = 32
HDIM = 24
KERN = 128
TFREQ = 128
BIN = 1024


norm_eps = 1e-05
mask_fill = -1e30


def from_partner(block, axis, apart):
    count = lax.axis_size(axis)
    route = []
    for low in range(count):
        high = low | 1 << apart
        if high != low and high < count:
            route += [(low, high), (high, low)]
    return lax.ppermute(block, axis, route)


def layer_norm(values, norm_gain, norm_offset):
    center = values - jnp.mean(values, axis=-1, keepdims=True)
    spread = jnp.mean(center * center, axis=-1, keepdims=True)
    return center * lax.rsqrt(spread + norm_eps) * norm_gain + norm_offset


def time_features(time_values):
    half_count = TFREQ // 2
    frequency = jnp.exp(
        jnp.arange(half_count, dtype=jnp.float32) * (-math.log(10000.0) / half_count)
    )
    angles = (1000.0 * time_values)[:, None] * frequency[None, :]
    return jnp.concatenate([jnp.sin(angles), jnp.cos(angles)], axis=1)


def distances(place_rows, place_keys):
    differ = place_rows[:, :, None] - place_keys[:, None, :]
    return jnp.sqrt(jnp.sum(differ * differ, axis=0))


def gaussian(distance, kern_mean, kern_width):
    scaled = (distance[None] - kern_mean[:, None, None]) / kern_width[:, None, None]
    return jnp.exp(-0.5 * scaled * scaled) / (math.sqrt(2.0 * math.pi) * kern_width[:, None, None])


def outer_sum(left_rows, right_rows):
    return jnp.einsum("ra,rb->ab", left_rows, right_rows, preferred_element_type=jnp.float32)


def times_transposed(left_rows, weight_matrix):
    return jnp.einsum("rb,ab->ra", left_rows, weight_matrix, preferred_element_type=jnp.float32)


def shards(
    atoms,
    positions,
    segment,
    item_time,
    time_weight,
    norm1_gain,
    norm1_bias,
    qkv_weight,
    out_weight,
    norm2_gain,
    norm2_bias,
    ffn_in,
    ffn_in_bias,
    ffn_out,
    ffn_out_bias,
    pair_weight,
    kernel_mean,
    kernel_width,
    cotangent,
):
    f32 = jnp.float32
    bf16 = jnp.bfloat16
    row_count = atoms.shape[0]
    gathered = (
        lax.all_gather(time_weight, ("grp", "dev"), axis=1, tiled=True),
        lax.all_gather(norm1_gain, ("grp", "dev"), axis=0, tiled=True),
        lax.all_gather(norm1_bias, ("grp", "dev"), axis=0, tiled=True),
        lax.all_gather(qkv_weight, ("grp", "dev"), axis=0, tiled=True),
        lax.all_gather(out_weight, ("grp", "dev"), axis=0, tiled=True),
        lax.all_gather(norm2_gain, ("grp", "dev"), axis=0, tiled=True),
        lax.all_gather(norm2_bias, ("grp", "dev"), axis=0, tiled=True),
        lax.all_gather(ffn_in, ("grp", "dev"), axis=0, tiled=True),
        lax.all_gather(ffn_in_bias, ("grp", "dev"), axis=0, tiled=True),
        lax.all_gather(ffn_out, ("grp", "dev"), axis=0, tiled=True),
        lax.all_gather(ffn_out_bias, ("grp", "dev"), axis=0, tiled=True),
    )
    (
        w_time,
        gain_one,
        shift_one,
        w_qkv,
        w_out,
        gain_two,
        shift_two,
        w_in,
        bias_in,
        w_back,
        bias_back,
    ) = gathered
    features = time_features(item_time).astype(bf16)
    stream_zero = atoms.astype(f32) + jnp.dot(features, w_time, preferred_element_type=f32)
    normed = layer_norm(stream_zero, gain_one.astype(f32), shift_one.astype(f32)).astype(bf16)
    packed = jnp.dot(normed, w_qkv, preferred_element_type=f32).astype(bf16)
    query = packed[:, :D]
    key_value = packed[:, D:]
    labels = segment.astype(f32)
    bit_count = (BIN // row_count).bit_length() - 1
    my_index = lax.axis_index("dev")
    kv_bin, places_bin, labels_bin = (key_value, positions, labels)
    for bit_index in range(bit_count):
        is_upper = my_index >> bit_index & 1 == 1
        other_kv = from_partner(kv_bin, "dev", bit_index)
        other_places, other_labels = from_partner((places_bin, labels_bin), "dev", bit_index)
        kv_bin = jnp.where(
            is_upper, jnp.concatenate([other_kv, kv_bin], 0), jnp.concatenate([kv_bin, other_kv], 0)
        )
        places_bin = jnp.where(
            is_upper,
            jnp.concatenate([other_places, places_bin], 1),
            jnp.concatenate([places_bin, other_places], 1),
        )
        labels_bin = jnp.where(
            is_upper,
            jnp.concatenate([other_labels, labels_bin], 0),
            jnp.concatenate([labels_bin, other_labels], 0),
        )
    block_rows = min(64, row_count)
    turns = row_count // block_rows
    scale = HDIM ** (-0.5)
    key_heads = kv_bin[:, :D].reshape(BIN, HEADS, HDIM)
    value_heads = kv_bin[:, D:].reshape(BIN, HEADS, HDIM)
    query_blocks = query.reshape(turns, block_rows, HEADS, HDIM)
    place_blocks = positions.reshape(3, turns, block_rows).transpose(1, 0, 2)
    label_blocks = labels.reshape(turns, block_rows)

    def block_scores(query_part, place_part, label_part):
        distance = distances(place_part, places_bin)
        kernels_low = gaussian(distance, kernel_mean, kernel_width).astype(bf16)
        bias_heads = jnp.einsum("kij,kh->hij", kernels_low, pair_weight, preferred_element_type=f32)
        raw_scores = (
            jnp.einsum("ihd,jhd->hij", query_part, key_heads, preferred_element_type=f32) * scale
            + bias_heads
        )
        same_item = label_part[:, None] == labels_bin[None, :]
        return (jnp.where(same_item[None], raw_scores, mask_fill), distance, kernels_low)

    def forward_block(state_unused, pieces):
        scores = block_scores(pieces[0], pieces[1], pieces[2])[0]
        top_score = jnp.max(scores, axis=-1, keepdims=True)
        shifted = jnp.exp(scores - top_score)
        row_total = jnp.sum(shifted, axis=-1, keepdims=True)
        weights = (shifted / row_total).astype(bf16)
        mixed_part = jnp.einsum("hij,jhd->ihd", weights, value_heads, preferred_element_type=f32)
        return (
            state_unused,
            (mixed_part.reshape(block_rows, D), (top_score + jnp.log(row_total))[:, :, 0]),
        )

    _, (mixed_blocks, log_totals) = lax.scan(
        forward_block, jnp.zeros((), f32), (query_blocks, place_blocks, label_blocks)
    )
    mixed_low = mixed_blocks.reshape(row_count, D).astype(bf16)
    stream_one = stream_zero + jnp.dot(mixed_low, w_out, preferred_element_type=f32)
    second = layer_norm(stream_one, gain_two.astype(f32), shift_two.astype(f32)).astype(bf16)
    hidden_pre = jnp.dot(second, w_in, preferred_element_type=f32) + bias_in.astype(f32)
    hidden_act = jax.nn.gelu(hidden_pre, approximate=False).astype(bf16)
    output = (
        stream_one + jnp.dot(hidden_act, w_back, preferred_element_type=f32) + bias_back.astype(f32)
    ).astype(bf16)
    again = (
        lax.all_gather(time_weight, ("grp", "dev"), axis=1, tiled=True),
        lax.all_gather(norm1_gain, ("grp", "dev"), axis=0, tiled=True),
        lax.all_gather(norm1_bias, ("grp", "dev"), axis=0, tiled=True),
        lax.all_gather(qkv_weight, ("grp", "dev"), axis=0, tiled=True),
        lax.all_gather(out_weight, ("grp", "dev"), axis=0, tiled=True),
        lax.all_gather(norm2_gain, ("grp", "dev"), axis=0, tiled=True),
        lax.all_gather(norm2_bias, ("grp", "dev"), axis=0, tiled=True),
        lax.all_gather(ffn_in, ("grp", "dev"), axis=0, tiled=True),
        lax.all_gather(ffn_in_bias, ("grp", "dev"), axis=0, tiled=True),
        lax.all_gather(ffn_out, ("grp", "dev"), axis=0, tiled=True),
        lax.all_gather(ffn_out_bias, ("grp", "dev"), axis=0, tiled=True),
    )
    (
        w_time,
        gain_one,
        shift_one,
        w_qkv,
        w_out,
        gain_two,
        shift_two,
        w_in,
        bias_in,
        w_back,
        bias_back,
    ) = again
    grad_output = cotangent.astype(f32)
    grad_branch = grad_output.astype(bf16)
    grad_back = outer_sum(hidden_act, grad_branch)
    grad_bias_back = jnp.sum(grad_branch.astype(f32), axis=0)
    grad_act = times_transposed(grad_branch, w_back)
    _, gelu_pull = jax.vjp(partial(jax.nn.gelu, approximate=False), hidden_pre)
    grad_pre = gelu_pull(grad_act)[0].astype(bf16)
    grad_in = outer_sum(second, grad_pre)
    grad_bias_in = jnp.sum(grad_pre.astype(f32), axis=0)
    grad_second = times_transposed(grad_pre, w_in)
    _, norm_two_pull = jax.vjp(layer_norm, stream_one, gain_two.astype(f32), shift_two.astype(f32))
    grad_stream_part, grad_gain_two, grad_shift_two = norm_two_pull(grad_second)
    grad_stream_one = grad_output + grad_stream_part
    grad_attn = grad_stream_one.astype(bf16)
    grad_out_weight = outer_sum(mixed_low, grad_attn)
    grad_mixed = times_transposed(grad_attn, w_out).astype(bf16)
    grad_blocks = grad_mixed.reshape(turns, block_rows, HEADS, HDIM)

    def backward_block(state, pieces):
        grad_keys, grad_values, grad_pair, grad_mean, grad_width = state
        query_part, place_part, label_part, log_part, grad_part = pieces
        scores, distance, kernels_low = block_scores(query_part, place_part, label_part)
        probs = jnp.exp(scores - log_part[:, :, None])
        grad_probs = jnp.einsum("ihd,jhd->hij", grad_part, value_heads, preferred_element_type=f32)
        inner = jnp.sum(probs * grad_probs, axis=-1, keepdims=True)
        grad_scores = (probs * (grad_probs - inner)).astype(bf16)
        grad_query = (
            jnp.einsum("hij,jhd->ihd", grad_scores, key_heads, preferred_element_type=f32) * scale
        )
        grad_keys = (
            grad_keys
            + jnp.einsum("hij,ihd->jhd", grad_scores, query_part, preferred_element_type=f32)
            * scale
        )
        grad_values = grad_values + jnp.einsum(
            "hij,ihd->jhd", probs.astype(bf16), grad_part, preferred_element_type=f32
        )
        grad_pair = grad_pair + jnp.einsum(
            "kij,hij->kh", kernels_low, grad_scores, preferred_element_type=f32
        )
        grad_kernels = jnp.einsum(
            "hij,kh->kij", grad_scores, pair_weight, preferred_element_type=f32
        )
        _, kernel_pull = jax.vjp(
            lambda mean_in, width_in: gaussian(distance, mean_in, width_in),
            kernel_mean,
            kernel_width,
        )
        mean_part, width_part = kernel_pull(grad_kernels)
        return (
            (grad_keys, grad_values, grad_pair, grad_mean + mean_part, grad_width + width_part),
            grad_query.reshape(block_rows, D),
        )

    start_state = (
        jnp.zeros((BIN, HEADS, HDIM), f32),
        jnp.zeros((BIN, HEADS, HDIM), f32),
        jnp.zeros((KERN, HEADS), f32),
        jnp.zeros((KERN,), f32),
        jnp.zeros((KERN,), f32),
    )
    (grad_keys, grad_values, grad_pair, grad_mean, grad_width), grad_query = lax.scan(
        backward_block,
        start_state,
        (query_blocks, place_blocks, label_blocks, log_totals, grad_blocks),
    )
    grad_bin = jnp.concatenate([grad_keys.reshape(BIN, D), grad_values.reshape(BIN, D)], axis=1)
    for bit_index in reversed(range(bit_count)):
        half_rows = grad_bin.shape[0] // 2
        is_upper = my_index >> bit_index & 1 == 1
        low_half = grad_bin[:half_rows]
        high_half = grad_bin[half_rows:]
        kept_half = jnp.where(is_upper, high_half, low_half)
        sent_half = jnp.where(is_upper, low_half, high_half)
        grad_bin = kept_half + from_partner(
            sent_half.astype(jnp.bfloat16), "dev", bit_index
        ).astype(sent_half.dtype)
    grad_packed = jnp.concatenate([grad_query.reshape(row_count, D), grad_bin], axis=1).astype(bf16)
    grad_qkv = outer_sum(normed, grad_packed)
    grad_normed = times_transposed(grad_packed, w_qkv)
    _, norm_one_pull = jax.vjp(layer_norm, stream_zero, gain_one.astype(f32), shift_one.astype(f32))
    grad_zero_part, grad_gain_one, grad_shift_one = norm_one_pull(grad_normed)
    grad_input = grad_stream_one + grad_zero_part
    grad_time = outer_sum(features, grad_input.astype(bf16))
    summed = (
        lax.psum_scatter(grad_time, ("grp", "dev"), scatter_dimension=1, tiled=True),
        lax.psum_scatter(grad_gain_one, ("grp", "dev"), scatter_dimension=0, tiled=True),
        lax.psum_scatter(grad_shift_one, ("grp", "dev"), scatter_dimension=0, tiled=True),
        lax.psum_scatter(grad_qkv, ("grp", "dev"), scatter_dimension=0, tiled=True),
        lax.psum_scatter(grad_out_weight, ("grp", "dev"), scatter_dimension=0, tiled=True),
        lax.psum_scatter(grad_gain_two, ("grp", "dev"), scatter_dimension=0, tiled=True),
        lax.psum_scatter(grad_shift_two, ("grp", "dev"), scatter_dimension=0, tiled=True),
        lax.psum_scatter(grad_in, ("grp", "dev"), scatter_dimension=0, tiled=True),
        lax.psum_scatter(grad_bias_in, ("grp", "dev"), scatter_dimension=0, tiled=True),
        lax.psum_scatter(grad_back, ("grp", "dev"), scatter_dimension=0, tiled=True),
        lax.psum_scatter(grad_bias_back, ("grp", "dev"), scatter_dimension=0, tiled=True),
    )
    pair_sums = lax.psum((grad_pair, grad_mean, grad_width), ("grp", "dev"))
    return (
        output,
        grad_input,
        summed[0],
        summed[1],
        summed[2],
        summed[3],
        summed[4],
        summed[5],
        summed[6],
        summed[7],
        summed[8],
        summed[9],
        summed[10],
        pair_sums[0],
        pair_sums[1],
        pair_sums[2],
    )


def solution(mesh):
    in_specs = (
        P(("grp", "dev"), None),
        P(None, ("grp", "dev")),
        P(("grp", "dev")),
        P(("grp", "dev")),
        P(None, ("grp", "dev")),
        P(("grp", "dev")),
        P(("grp", "dev")),
        P(("grp", "dev"), None),
        P(("grp", "dev"), None),
        P(("grp", "dev")),
        P(("grp", "dev")),
        P(("grp", "dev"), None),
        P(("grp", "dev")),
        P(("grp", "dev"), None),
        P(("grp", "dev")),
        P(),
        P(),
        P(),
        P(("grp", "dev"), None),
    )
    out_specs = (
        P(("grp", "dev"), None),
        P(("grp", "dev"), None),
        P(None, ("grp", "dev")),
        P(("grp", "dev")),
        P(("grp", "dev")),
        P(("grp", "dev"), None),
        P(("grp", "dev"), None),
        P(("grp", "dev")),
        P(("grp", "dev")),
        P(("grp", "dev"), None),
        P(("grp", "dev")),
        P(("grp", "dev"), None),
        P(("grp", "dev")),
        P(),
        P(),
        P(),
    )
    return jax.shard_map(shards, mesh=mesh, in_specs=in_specs, out_specs=out_specs, check_vma=False)
```

profile of v0, /device:TPU:0, one launch (start us, length us, event | category | flops | bytes accessed | tf_op | source)
XLA Modules:
  0.0 1407.2 jit_solution(7936561606452383695)
XLA Ops:
  14.5 42.5 %all-reduce.14 = (bf16[768]{0:T(1024)(128)(2,1)S(1)}, bf16[768]{0:T(1024)(128)(2,1)S(1)}, bf16[3072]{0:T(1024)(128)(2,1)S(1)}, bf16[768]{0:T(1024)(128)(2,1)}, b...) all-reduce(bf16[768]{0:T(1024)(128)(2,1)S(1)} %dynamic-update-slice.1,, ...), channel_id=1, replica_groups=mesh['grp'=4,'dev'=8] {'grp','dev'}, use_global_device_ids=true, to_apply=%add.1 | all-reduce | flops 6912 | bytes 27648
  57.0 41.6 %all_gather.39 = bf16[128,768]{0,1:T(8,128)(2,1)S(1)} all-gather(bf16[128,24]{0,1:T(8,128)(2,1)} %param.27), channel_id=1, replica_groups=mesh['grp'=4,'dev'=8] {'grp','dev'}, dimensions={1}, use_global_device_ids=true | all-gather | bytes 202752 | tf_op jit(solution)/shard_map/all_gather | solution.py:89
  118.1 31.5 %collective-permute-done.1 = f32[512]{0:T(512)S(1)} collective-permute-done((f32[512]{0:T(512)S(1)}, f32[512]{0:T(512)S(1)}, u32[]{:S(2)}, u32[]{:S(2)}) %collective-permute-start.1) | collective-permute-done | bytes 2080 | tf_op jit(solution)/shard_map/ppermute | solution.py:28
  158.7 97.8 %while.34 = (s32[]{:T(128)}, bf16[4,64,768]{2,1,0:T(8,128)(2,1)}, f32[4,32,64]{2,1,0:T(8,128)}, f32[4,64]{1,0:T(4,128)}, f32[1024]{0:T(1024)S(1)}, /*index=5*/bf...) while((s32[]{:T(128)}, bf16[4,64,768]{2,1,0:T(8,128)(2,1)}, ...), condition=%wide.region_6.7_spmd, body=%wide.region_2.6_spmd.sunk | while | flops 807991424 | bytes 47060640 | solution.py:173
  160.9 9.8 fusion.145
  170.7 8.1 fusion.147
  185.2 9.8 fusion.145
  195.0 8.1 fusion.147
  209.4 9.8 fusion.145
  219.3 8.1 fusion.147
  233.7 9.8 fusion.145
  243.6 8.1 fusion.147
  261.1 5.7 convolution_add_fusion
  266.9 12.2 convert_reduce_fusion
  290.1 456.5 %while.35 = (s32[]{:T(128)}, f32[1024,32,24]{0,2,1:T(8,128)}, f32[1024,32,24]{0,2,1:T(8,128)}, f32[128,32]{0,1:T(8,128)}, f32[128]{0:T(128)}, /*index=5*/f32[128...) while((s32[]{:T(128)}, f32[1024,32,24]{0,2,1:T(8,128)}, ...), condition=%wide.region_17.18_spmd.clone, body=%wide.region_11.17_spmd.clone.sunk | while | flops 2424740864 | bytes 314550080 | solution.py:271
  298.2 17.3 %fusion.162 = f32[64,1024,32]{1,2,0:T(8,128)} fusion(f32[128]{0:T(128)S(1)} %get-tuple-element.837, f32[128]{0:T(128)S(1)} %copy-done.65, f32[128]{0:T(128)S(1)} %copy-done.62, f32[64,1024]{1,0:T(8,128)S(1)} %sqrt.19, bf16[128,32]{0,1:T(8,128)(2,1)S(1)} %copy-done.83), kind=kOutput, calls=%fused_computation.37.clone.1 | convolution fusion | flops 587202560 | bytes 8660480 | tf_op jit(solution)/shard_map/while/body/eval_jaxpr/kij,kh->hij/dot_general | solution.py:153
  315.4 10.9 multiply_reduce_fusion.14
  330.6 17.2 %fusion.164 = f32[128,32]{0,1:T(8,128)S(1)} fusion(f32[128]{0:T(128)S(1)} %get-tuple-element.837, f32[128]{0:T(128)S(1)} %copy-done.65, f32[128]{0:T(128)S(1)} %copy-done.62, f32[64,1024]{1,0:T(8,128)S(1)} %sqrt.19, bf16[32,64,1024]{2,1,0:T(8,128)(2,1)S(1)} %multiply_convert_fusion.3, f32[128,32]{0,1:T(8,128)S(1)} %copy-done.53, pred[]{:T(512)S(6)} %compare.3), kind=kOutput, calls=%fused_computation.53.clone.1 | convolution fusion | flops 587210752 | bytes 4490753 | tf_op jit(solution)/shard_map/while/body/eval_jaxpr/kij,hij->kh/dot_general | solution.py:247
  354.9 26.9 %fusion.165 = (f32[128,64,1024]{0,2,1:T(8,128)}, f32[64,1024,128]{2,1,0:T(8,128)}) fusion(f32[128]{0:T(128)S(1)} %get-tuple-element.837, f32[128]{0:T(128)S(1)} %copy-done.65, f32[128]{0:T(128)S(1)} %copy-done.62, f32[64,1024]{1,0:T(8,128)S(1)} %sqrt.19, bf16[128,32]{0,1:T(8,128)(2,1)S(1)} %copy-done.83, bf16[32,64,1024]{2,1,0:T(8,128)(2,1)S(1)} %copy-done.1), kind=kOutput, calls=%fused_computation.30.clone.1 | convolution fusion | flops 620756992 | bytes 71575040 | tf_op jit(solution)/shard_map/while/body/eval_jaxpr/hij,kh->kij/dot_general | solution.py:250
  381.8 21.2 %fusion.166 = (f32[128]{0:T(128)S(1)}, f32[128]{0:T(128)S(1)}, f32[128]{0:T(128)S(1)}) fusion(f32[128,64,1024]{0,2,1:T(8,128)} %get-tuple-element.840, f32[128]{0:T(128)S(1)} %copy-done.66, f32[128]{0:T(128)S(1)} %copy-done.62, f32[64,1024]{1,0:T(8,128)S(1)} %sqrt.19, f32[128]{0:T(128)S(1)} %copy-done.65, f32[64,1024,128]{2,1,0:T(8,128)} %get-tuple-element.841, ...), kind=kLoop, calls=%fused_computation.28.clone.1 | loop fusion | flops 100662912 | bytes 67374592 | tf_op jit(solution)/shard_map/while/body/eval_jaxpr/transpose(jvp())/reduce_sum | solution.py:52
  411.4 17.3 %fusion.162 = f32[64,1024,32]{1,2,0:T(8,128)} fusion(f32[128]{0:T(128)S(1)} %get-tuple-element.837, f32[128]{0:T(128)S(1)} %copy-done.65, f32[128]{0:T(128)S(1)} %copy-done.62, f32[64,1024]{1,0:T(8,128)S(1)} %sqrt.19, bf16[128,32]{0,1:T(8,128)(2,1)S(1)} %copy-done.83), kind=kOutput, calls=%fused_computation.37.clone.1 | convolution fusion | flops 587202560 | bytes 8660480 | tf_op jit(solution)/shard_map/while/body/eval_jaxpr/kij,kh->hij/dot_general | solution.py:153
  428.7 10.9 multiply_reduce_fusion.14
  443.8 17.2 %fusion.164 = f32[128,32]{0,1:T(8,128)S(1)} fusion(f32[128]{0:T(128)S(1)} %get-tuple-element.837, f32[128]{0:T(128)S(1)} %copy-done.65, f32[128]{0:T(128)S(1)} %copy-done.62, f32[64,1024]{1,0:T(8,128)S(1)} %sqrt.19, bf16[32,64,1024]{2,1,0:T(8,128)(2,1)S(1)} %multiply_convert_fusion.3, f32[128,32]{0,1:T(8,128)S(1)} %copy-done.53, pred[]{:T(512)S(6)} %compare.3), kind=kOutput, calls=%fused_computation.53.clone.1 | convolution fusion | flops 587210752 | bytes 4490753 | tf_op jit(solution)/shard_map/while/body/eval_jaxpr/kij,hij->kh/dot_general | solution.py:247
  463.1 6.0 bitcast_add_fusion.6
  469.2 26.9 %fusion.165 = (f32[128,64,1024]{0,2,1:T(8,128)}, f32[64,1024,128]{2,1,0:T(8,128)}) fusion(f32[128]{0:T(128)S(1)} %get-tuple-element.837, f32[128]{0:T(128)S(1)} %copy-done.65, f32[128]{0:T(128)S(1)} %copy-done.62, f32[64,1024]{1,0:T(8,128)S(1)} %sqrt.19, bf16[128,32]{0,1:T(8,128)(2,1)S(1)} %copy-done.83, bf16[32,64,1024]{2,1,0:T(8,128)(2,1)S(1)} %copy-done.1), kind=kOutput, calls=%fused_computation.30.clone.1 | convolution fusion | flops 620756992 | bytes 71575040 | tf_op jit(solution)/shard_map/while/body/eval_jaxpr/hij,kh->kij/dot_general | solution.py:250
  496.1 21.2 %fusion.166 = (f32[128]{0:T(128)S(1)}, f32[128]{0:T(128)S(1)}, f32[128]{0:T(128)S(1)}) fusion(f32[128,64,1024]{0,2,1:T(8,128)} %get-tuple-element.840, f32[128]{0:T(128)S(1)} %copy-done.66, f32[128]{0:T(128)S(1)} %copy-done.62, f32[64,1024]{1,0:T(8,128)S(1)} %sqrt.19, f32[128]{0:T(128)S(1)} %copy-done.65, f32[64,1024,128]{2,1,0:T(8,128)} %get-tuple-element.841, ...), kind=kLoop, calls=%fused_computation.28.clone.1 | loop fusion | flops 100662912 | bytes 67374592 | tf_op jit(solution)/shard_map/while/body/eval_jaxpr/transpose(jvp())/reduce_sum | solution.py:52
  525.7 17.3 %fusion.162 = f32[64,1024,32]{1,2,0:T(8,128)} fusion(f32[128]{0:T(128)S(1)} %get-tuple-element.837, f32[128]{0:T(128)S(1)} %copy-done.65, f32[128]{0:T(128)S(1)} %copy-done.62, f32[64,1024]{1,0:T(8,128)S(1)} %sqrt.19, bf16[128,32]{0,1:T(8,128)(2,1)S(1)} %copy-done.83), kind=kOutput, calls=%fused_computation.37.clone.1 | convolution fusion | flops 587202560 | bytes 8660480 | tf_op jit(solution)/shard_map/while/body/eval_jaxpr/kij,kh->hij/dot_general | solution.py:153
  543.0 10.9 multiply_reduce_fusion.14
  558.1 17.2 %fusion.164 = f32[128,32]{0,1:T(8,128)S(1)} fusion(f32[128]{0:T(128)S(1)} %get-tuple-element.837, f32[128]{0:T(128)S(1)} %copy-done.65, f32[128]{0:T(128)S(1)} %copy-done.62, f32[64,1024]{1,0:T(8,128)S(1)} %sqrt.19, bf16[32,64,1024]{2,1,0:T(8,128)(2,1)S(1)} %multiply_convert_fusion.3, f32[128,32]{0,1:T(8,128)S(1)} %copy-done.53, pred[]{:T(512)S(6)} %compare.3), kind=kOutput, calls=%fused_computation.53.clone.1 | convolution fusion | flops 587210752 | bytes 4490753 | tf_op jit(solution)/shard_map/while/body/eval_jaxpr/kij,hij->kh/dot_general | solution.py:247
  577.4 6.0 bitcast_add_fusion.6
  583.4 26.9 %fusion.165 = (f32[128,64,1024]{0,2,1:T(8,128)}, f32[64,1024,128]{2,1,0:T(8,128)}) fusion(f32[128]{0:T(128)S(1)} %get-tuple-element.837, f32[128]{0:T(128)S(1)} %copy-done.65, f32[128]{0:T(128)S(1)} %copy-done.62, f32[64,1024]{1,0:T(8,128)S(1)} %sqrt.19, bf16[128,32]{0,1:T(8,128)(2,1)S(1)} %copy-done.83, bf16[32,64,1024]{2,1,0:T(8,128)(2,1)S(1)} %copy-done.1), kind=kOutput, calls=%fused_computation.30.clone.1 | convolution fusion | flops 620756992 | bytes 71575040 | tf_op jit(solution)/shard_map/while/body/eval_jaxpr/hij,kh->kij/dot_general | solution.py:250
  610.3 21.2 %fusion.166 = (f32[128]{0:T(128)S(1)}, f32[128]{0:T(128)S(1)}, f32[128]{0:T(128)S(1)}) fusion(f32[128,64,1024]{0,2,1:T(8,128)} %get-tuple-element.840, f32[128]{0:T(128)S(1)} %copy-done.66, f32[128]{0:T(128)S(1)} %copy-done.62, f32[64,1024]{1,0:T(8,128)S(1)} %sqrt.19, f32[128]{0:T(128)S(1)} %copy-done.65, f32[64,1024,128]{2,1,0:T(8,128)} %get-tuple-element.841, ...), kind=kLoop, calls=%fused_computation.28.clone.1 | loop fusion | flops 100662912 | bytes 67374592 | tf_op jit(solution)/shard_map/while/body/eval_jaxpr/transpose(jvp())/reduce_sum | solution.py:52
  640.0 17.3 %fusion.162 = f32[64,1024,32]{1,2,0:T(8,128)} fusion(f32[128]{0:T(128)S(1)} %get-tuple-element.837, f32[128]{0:T(128)S(1)} %copy-done.65, f32[128]{0:T(128)S(1)} %copy-done.62, f32[64,1024]{1,0:T(8,128)S(1)} %sqrt.19, bf16[128,32]{0,1:T(8,128)(2,1)S(1)} %copy-done.83), kind=kOutput, calls=%fused_computation.37.clone.1 | convolution fusion | flops 587202560 | bytes 8660480 | tf_op jit(solution)/shard_map/while/body/eval_jaxpr/kij,kh->hij/dot_general | solution.py:153
  657.2 10.9 multiply_reduce_fusion.14
  672.4 17.2 %fusion.164 = f32[128,32]{0,1:T(8,128)S(1)} fusion(f32[128]{0:T(128)S(1)} %get-tuple-element.837, f32[128]{0:T(128)S(1)} %copy-done.65, f32[128]{0:T(128)S(1)} %copy-done.62, f32[64,1024]{1,0:T(8,128)S(1)} %sqrt.19, bf16[32,64,1024]{2,1,0:T(8,128)(2,1)S(1)} %multiply_convert_fusion.3, f32[128,32]{0,1:T(8,128)S(1)} %copy-done.53, pred[]{:T(512)S(6)} %compare.3), kind=kOutput, calls=%fused_computation.53.clone.1 | convolution fusion | flops 587210752 | bytes 4490753 | tf_op jit(solution)/shard_map/while/body/eval_jaxpr/kij,hij->kh/dot_general | solution.py:247
  691.7 6.0 bitcast_add_fusion.6
  697.7 26.9 %fusion.165 = (f32[128,64,1024]{0,2,1:T(8,128)}, f32[64,1024,128]{2,1,0:T(8,128)}) fusion(f32[128]{0:T(128)S(1)} %get-tuple-element.837, f32[128]{0:T(128)S(1)} %copy-done.65, f32[128]{0:T(128)S(1)} %copy-done.62, f32[64,1024]{1,0:T(8,128)S(1)} %sqrt.19, bf16[128,32]{0,1:T(8,128)(2,1)S(1)} %copy-done.83, bf16[32,64,1024]{2,1,0:T(8,128)(2,1)S(1)} %copy-done.1), kind=kOutput, calls=%fused_computation.30.clone.1 | convolution fusion | flops 620756992 | bytes 71575040 | tf_op jit(solution)/shard_map/while/body/eval_jaxpr/hij,kh->kij/dot_general | solution.py:250
  724.6 21.2 %fusion.166 = (f32[128]{0:T(128)S(1)}, f32[128]{0:T(128)S(1)}, f32[128]{0:T(128)S(1)}) fusion(f32[128,64,1024]{0,2,1:T(8,128)} %get-tuple-element.840, f32[128]{0:T(128)S(1)} %copy-done.66, f32[128]{0:T(128)S(1)} %copy-done.62, f32[64,1024]{1,0:T(8,128)S(1)} %sqrt.19, f32[128]{0:T(128)S(1)} %copy-done.65, f32[64,1024,128]{2,1,0:T(8,128)} %get-tuple-element.841, ...), kind=kLoop, calls=%fused_computation.28.clone.1 | loop fusion | flops 100662912 | bytes 67374592 | tf_op jit(solution)/shard_map/while/body/eval_jaxpr/transpose(jvp())/reduce_sum | solution.py:52
  750.9 35.2 %collective-permute-done.6 = bf16[512,1536]{0,1:T(8,128)(2,1)S(1)} collective-permute-done((bf16[512,1536]{0,1:T(8,128)(2,1)S(1)}, bf16[512,1536]{0,1:T(8,128)(2,1)S(1)}, u32[]{:S(2)}, u32[]{:S(2)}) %collective-permute-start.6) | collective-permute-done | bytes 1572896 | tf_op jit(solution)/shard_map/ppermute | solution.py:28
  798.0 5.2 fusion.65
  805.0 5.2 fusion.78
  813.7 5.1 fusion.87
  824.1 37.9 %all-reduce.13 = (f32[768]{0:T(1024)S(1)}, f32[768]{0:T(1024)S(1)}, f32[768]{0:T(1024)S(1)}, f32[768]{0:T(1024)S(1)}, f32[3072]{0:T(1024)S(1)}, /*index=5*/f32[7...) all-reduce(f32[768]{0:T(1024)S(1)} %copy-done.77, ...), channel_id=3, replica_groups=mesh['grp'=4,'dev'=8] {'grp','dev'}, use_global_device_ids=true, to_apply=%region_22.23.clone | all-reduce | flops 11264 | bytes 90112
  865.5 22.0 %reduce-scatter.16.cloned.1.call-done = f32[128,24]{0,1:T(8,128)} async-done(((f32[128,768]{0,1:T(8,128)}), f32[128,24]{0,1:T(8,128)}) %reduce-scatter.16.cloned.1.call-update) | async-done | bytes 12304
  887.5 104.7 %reduce-scatter.10.cloned.1.call-done = f32[24,768]{1,0:T(8,128)} async-done(((f32[768,768]{1,0:T(8,128)}), f32[24,768]{1,0:T(8,128)}) %reduce-scatter.10.cloned.1.call-update) | async-done | bytes 73744 | tf_op jit(solution)/shard_map/reduce_scatter | solution.py:299
  992.3 124.3 %reduce-scatter.8.cloned.1.call-done = f32[24,2304]{1,0:T(8,128)} async-done(((f32[768,2304]{1,0:T(8,128)}), f32[24,2304]{1,0:T(8,128)}) %reduce-scatter.8.cloned.1.call-update) | async-done | bytes 221200 | tf_op jit(solution)/shard_map/reduce_scatter | solution.py:298
  1116.6 142.4 %reduce-scatter.12.cloned.1.call-done = f32[24,3072]{1,0:T(8,128)} async-done(((f32[768,3072]{1,0:T(8,128)}), f32[24,3072]{1,0:T(8,128)}) %reduce-scatter.12.cloned.1.call-update) | async-done | bytes 294928 | tf_op jit(solution)/shard_map/reduce_scatter | solution.py:302
  1259.0 141.2 %reduce-scatter.14.cloned.1.call-done = f32[96,768]{1,0:T(8,128)} async-done(((f32[3072,768]{1,0:T(8,128)}), f32[96,768]{1,0:T(8,128)}) %reduce-scatter.14.cloned.1.call-update) | async-done | bytes 294928 | tf_op jit(solution)/shard_map/reduce_scatter | solution.py:304
  (509 shorter events, 169.3 us)
Async XLA Ops:
  7.2 94.7 %all-gather.5.cloned.1.call-start = ((), (), s32[]{:S(2)}) async-start(), calls=%async_computation.5 | async-start | bytes 3649536 | tf_op jit(solution)/shard_map/all_gather | solution.py:92
  7.9 248.6 %all-gather.7.cloned.1.call-start = ((), (), s32[]{:S(2)}) async-start(), calls=%async_computation.6 | async-start | bytes 1216512 | tf_op jit(solution)/shard_map/all_gather | solution.py:93
  8.7 252.4 %all-gather.9.cloned.1.call-start = ((), (), s32[]{:S(2)}) async-start(), calls=%async_computation.7 | async-start | bytes 4866048 | tf_op jit(solution)/shard_map/all_gather | solution.py:96
  9.4 257.4 %all-gather.11.cloned.1.call-start = ((), (), s32[]{:S(2)}) async-start(), calls=%async_computation.8 | async-start | bytes 4866048 | tf_op jit(solution)/shard_map/all_gather | solution.py:98
  57.0 48.1 %copy-start.39 = (f32[768]{0:T(1024)}, f32[768]{0:T(1024)S(1)}, u32[]{:S(2)}) copy-start(f32[768]{0:T(1024)S(1)} %convert_element_type.102) | copy-start | bytes 9220
  57.0 48.1 %copy-start.35 = (f32[768]{0:T(1024)}, f32[768]{0:T(1024)S(1)}, u32[]{:S(2)}) copy-start(f32[768]{0:T(1024)S(1)} %convert_element_type.101) | copy-start | bytes 9220
  105.2 2.5 collective-permute-start.2
  109.5 42.2 %collective-permute-start.3 = (bf16[512,1536]{1,0:T(8,128)(2,1)S(1)}, bf16[512,1536]{1,0:T(8,128)(2,1)}, u32[]{:S(2)}, u32[]{:S(2)}) collective-permute-start(bf16[512,1536]{1,0:T(8,128)(2,1)S(1)} %maximum_select_fusion.1), channel_id=1, source_target_pairs={{0,2},{2,0},{1,3},{3,1},{4,6},{6,4},{5,7},{7,5},{8,10},{10,8},{9,1... | collective-permute-start | bytes 4718600 | tf_op jit(solution)/shard_map/ppermute | solution.py:28
  110.3 5.6 collective-permute-start
  110.6 7.4 collective-permute-start.4
  110.8 776.7 %reduce-scatter.16.cloned.1.call-start = ((), (), s32[]{:S(2)}) async-start(), calls=%async_computation.13 | async-start | bytes 405504
  115.9 33.7 %collective-permute-start.1 = (f32[512]{0:T(512)S(1)}, f32[512]{0:T(512)S(1)}, u32[]{:S(2)}, u32[]{:S(2)}) collective-permute-start(f32[512]{0:T(512)S(1)} %maximum_select_fusion.5), channel_id=1, source_target_pairs={{0,2},{2,0},{1,3},{3,1},{4,6},{6,4},{5,7},{7,5},{8,10},{10,8},{9,1... | collective-permute-start | bytes 6152 | tf_op jit(solution)/shard_map/ppermute | solution.py:28
  118.0 32.2 %collective-permute-start.5 = (f32[3,512]{1,0:T(4,128)S(1)}, f32[3,512]{1,0:T(4,128)S(1)}, u32[]{:S(2)}, u32[]{:S(2)}) collective-permute-start(f32[3,512]{1,0:T(4,128)S(1)} %maximum_select_fusion.3), channel_id=1, source_target_pairs={{0,2},{2,0},{1,3},{3,1},{4,6},{6,4},{5,7},{7,5},{8,10},{10,8},{9,1... | collective-permute-start | bytes 18440 | tf_op jit(solution)/shard_map/ppermute | solution.py:28
  354.9 26.9 %copy-start.66 = (f32[128]{0:T(128)S(1)}, f32[128]{0:T(128)}, u32[]{:S(2)}) copy-start(f32[128]{0:T(128)} %divide_bitcast_fusion.2) | copy-start | bytes 1540 | tf_op jit(solution)/shard_map/while
  354.9 26.9 %copy-start.67 = (f32[128]{0:T(128)S(1)}, f32[128]{0:T(128)}, u32[]{:S(2)}) copy-start(f32[128]{0:T(128)} %get-tuple-element.842) | copy-start | bytes 1540 | tf_op jit(solution)/shard_map/while
  381.8 21.3 %copy-start.47 = (f32[128]{0:T(128)S(1)}, f32[128]{0:T(128)}, u32[]{:S(2)}) copy-start(f32[128]{0:T(128)} %get-tuple-element.917) | copy-start | bytes 1540 | tf_op jit(solution)/shard_map/while
  381.8 21.3 %copy-start.50 = (f32[128]{0:T(128)S(1)}, f32[128]{0:T(128)}, u32[]{:S(2)}) copy-start(f32[128]{0:T(128)} %get-tuple-element.916) | copy-start | bytes 1540 | tf_op jit(solution)/shard_map/while
  381.8 21.8 %copy-start.7 = (bf16[1024,32,24]{0,2,1:T(8,128)(2,1)S(1)}, bf16[1024,32,24]{0,2,1:T(8,128)(2,1)}, u32[]{:S(2)}) copy-start(bf16[1024,32,24]{0,2,1:T(8,128)(2,1)} %copy-done.6) | copy-start | bytes 4718596 | tf_op jit(solution)/shard_map/while
  381.8 21.8 %copy-start.26 = (f32[3,1024]{1,0:T(4,128)S(1)}, f32[3,1024]{1,0:T(4,128)}, u32[]{:S(2)}) copy-start(f32[3,1024]{1,0:T(4,128)} %copy-done.25) | copy-start | bytes 36868 | tf_op jit(solution)/shard_map/while
  441.5 19.6 %copy-start = (bf16[32,64,1024]{2,1,0:T(8,128)(2,1)}, bf16[32,64,1024]{2,1,0:T(8,128)(2,1)S(1)}, u32[]{:S(2)}) copy-start(bf16[32,64,1024]{2,1,0:T(8,128)(2,1)S(1)} %multiply_convert_fusion.3) | copy-start | bytes 12582916 | tf_op jit(solution)/shard_map/while
  469.1 26.9 %copy-start.66 = (f32[128]{0:T(128)S(1)}, f32[128]{0:T(128)}, u32[]{:S(2)}) copy-start(f32[128]{0:T(128)} %divide_bitcast_fusion.2) | copy-start | bytes 1540 | tf_op jit(solution)/shard_map/while
  469.1 26.9 %copy-start.67 = (f32[128]{0:T(128)S(1)}, f32[128]{0:T(128)}, u32[]{:S(2)}) copy-start(f32[128]{0:T(128)} %get-tuple-element.842) | copy-start | bytes 1540 | tf_op jit(solution)/shard_map/while
  496.0 21.3 %copy-start.47 = (f32[128]{0:T(128)S(1)}, f32[128]{0:T(128)}, u32[]{:S(2)}) copy-start(f32[128]{0:T(128)} %get-tuple-element.917) | copy-start | bytes 1540 | tf_op jit(solution)/shard_map/while
  496.0 21.3 %copy-start.50 = (f32[128]{0:T(128)S(1)}, f32[128]{0:T(128)}, u32[]{:S(2)}) copy-start(f32[128]{0:T(128)} %get-tuple-element.916) | copy-start | bytes 1540 | tf_op jit(solution)/shard_map/while
  496.0 21.8 %copy-start.7 = (bf16[1024,32,24]{0,2,1:T(8,128)(2,1)S(1)}, bf16[1024,32,24]{0,2,1:T(8,128)(2,1)}, u32[]{:S(2)}) copy-start(bf16[1024,32,24]{0,2,1:T(8,128)(2,1)} %copy-done.6) | copy-start | bytes 4718596 | tf_op jit(solution)/shard_map/while
  496.1 21.8 %copy-start.26 = (f32[3,1024]{1,0:T(4,128)S(1)}, f32[3,1024]{1,0:T(4,128)}, u32[]{:S(2)}) copy-start(f32[3,1024]{1,0:T(4,128)} %copy-done.25) | copy-start | bytes 36868 | tf_op jit(solution)/shard_map/while
  555.7 19.6 %copy-start = (bf16[32,64,1024]{2,1,0:T(8,128)(2,1)}, bf16[32,64,1024]{2,1,0:T(8,128)(2,1)S(1)}, u32[]{:S(2)}) copy-start(bf16[32,64,1024]{2,1,0:T(8,128)(2,1)S(1)} %multiply_convert_fusion.3) | copy-start | bytes 12582916 | tf_op jit(solution)/shard_map/while
  583.4 26.9 %copy-start.66 = (f32[128]{0:T(128)S(1)}, f32[128]{0:T(128)}, u32[]{:S(2)}) copy-start(f32[128]{0:T(128)} %divide_bitcast_fusion.2) | copy-start | bytes 1540 | tf_op jit(solution)/shard_map/while
  583.4 26.9 %copy-start.67 = (f32[128]{0:T(128)S(1)}, f32[128]{0:T(128)}, u32[]{:S(2)}) copy-start(f32[128]{0:T(128)} %get-tuple-element.842) | copy-start | bytes 1540 | tf_op jit(solution)/shard_map/while
  610.3 21.3 %copy-start.47 = (f32[128]{0:T(128)S(1)}, f32[128]{0:T(128)}, u32[]{:S(2)}) copy-start(f32[128]{0:T(128)} %get-tuple-element.917) | copy-start | bytes 1540 | tf_op jit(solution)/shard_map/while
  610.3 21.3 %copy-start.50 = (f32[128]{0:T(128)S(1)}, f32[128]{0:T(128)}, u32[]{:S(2)}) copy-start(f32[128]{0:T(128)} %get-tuple-element.916) | copy-start | bytes 1540 | tf_op jit(solution)/shard_map/while
  610.3 21.8 %copy-start.7 = (bf16[1024,32,24]{0,2,1:T(8,128)(2,1)S(1)}, bf16[1024,32,24]{0,2,1:T(8,128)(2,1)}, u32[]{:S(2)}) copy-start(bf16[1024,32,24]{0,2,1:T(8,128)(2,1)} %copy-done.6) | copy-start | bytes 4718596 | tf_op jit(solution)/shard_map/while
  610.3 21.8 %copy-start.26 = (f32[3,1024]{1,0:T(4,128)S(1)}, f32[3,1024]{1,0:T(4,128)}, u32[]{:S(2)}) copy-start(f32[3,1024]{1,0:T(4,128)} %copy-done.25) | copy-start | bytes 36868 | tf_op jit(solution)/shard_map/while
  670.0 19.6 %copy-start = (bf16[32,64,1024]{2,1,0:T(8,128)(2,1)}, bf16[32,64,1024]{2,1,0:T(8,128)(2,1)S(1)}, u32[]{:S(2)}) copy-start(bf16[32,64,1024]{2,1,0:T(8,128)(2,1)S(1)} %multiply_convert_fusion.3) | copy-start | bytes 12582916 | tf_op jit(solution)/shard_map/while
  697.7 26.9 %copy-start.66 = (f32[128]{0:T(128)S(1)}, f32[128]{0:T(128)}, u32[]{:S(2)}) copy-start(f32[128]{0:T(128)} %divide_bitcast_fusion.2) | copy-start | bytes 1540 | tf_op jit(solution)/shard_map/while
  697.7 26.9 %copy-start.67 = (f32[128]{0:T(128)S(1)}, f32[128]{0:T(128)}, u32[]{:S(2)}) copy-start(f32[128]{0:T(128)} %get-tuple-element.842) | copy-start | bytes 1540 | tf_op jit(solution)/shard_map/while
  724.6 21.3 %copy-start.47 = (f32[128]{0:T(128)S(1)}, f32[128]{0:T(128)}, u32[]{:S(2)}) copy-start(f32[128]{0:T(128)} %get-tuple-element.917) | copy-start | bytes 1540 | tf_op jit(solution)/shard_map/while
  724.6 21.3 %copy-start.50 = (f32[128]{0:T(128)S(1)}, f32[128]{0:T(128)}, u32[]{:S(2)}) copy-start(f32[128]{0:T(128)} %get-tuple-element.916) | copy-start | bytes 1540 | tf_op jit(solution)/shard_map/while
  724.6 21.8 %copy-start.7 = (bf16[1024,32,24]{0,2,1:T(8,128)(2,1)S(1)}, bf16[1024,32,24]{0,2,1:T(8,128)(2,1)}, u32[]{:S(2)}) copy-start(bf16[1024,32,24]{0,2,1:T(8,128)(2,1)} %copy-done.6) | copy-start | bytes 4718596 | tf_op jit(solution)/shard_map/while
  724.6 21.8 %copy-start.26 = (f32[3,1024]{1,0:T(4,128)S(1)}, f32[3,1024]{1,0:T(4,128)}, u32[]{:S(2)}) copy-start(f32[3,1024]{1,0:T(4,128)} %copy-done.25) | copy-start | bytes 36868 | tf_op jit(solution)/shard_map/while
  746.7 39.4 %copy-start.2 = (f32[1024,32,24]{0,2,1:T(8,128)S(1)}, f32[1024,32,24]{0,2,1:T(8,128)}, u32[]{:S(2)}) copy-start(f32[1024,32,24]{0,2,1:T(8,128)} %get-tuple-element.270) | copy-start | bytes 9437188
  746.7 39.4 %copy-start.5 = (f32[1024,32,24]{0,2,1:T(8,128)S(1)}, f32[1024,32,24]{0,2,1:T(8,128)}, u32[]{:S(2)}) copy-start(f32[1024,32,24]{0,2,1:T(8,128)} %get-tuple-element.271) | copy-start | bytes 9437188
  750.2 35.8 %collective-permute-start.6 = (bf16[512,1536]{0,1:T(8,128)(2,1)S(1)}, bf16[512,1536]{0,1:T(8,128)(2,1)S(1)}, u32[]{:S(2)}, u32[]{:S(2)}) collective-permute-start(bf16[512,1536]{0,1:T(8,128)(2,1)S(1)} %select_convert_fusion), channel_id=1, source_target_pairs={{0,2},{2,0},{1,3},{3,1},{4,6},{6,4},{5,7},{7,5},{8,10},{10,8},{9,1... | collective-permute-start | bytes 4718600 | tf_op jit(solution)/shard_map/ppermute | solution.py:28
  788.0 2.6 collective-permute-start.7
  796.0 196.3 %reduce-scatter.10.cloned.1.call-start = ((), (), s32[]{:S(2)}) async-start(), calls=%async_computation.10 | async-start | bytes 2433024 | tf_op jit(solution)/shard_map/reduce_scatter | solution.py:299
  798.0 318.7 %reduce-scatter.8.cloned.1.call-start = ((), (), s32[]{:S(2)}) async-start(), calls=%async_computation.9 | async-start | bytes 7299072 | tf_op jit(solution)/shard_map/reduce_scatter | solution.py:298
  803.3 455.7 %reduce-scatter.12.cloned.1.call-start = ((), (), s32[]{:S(2)}) async-start(), calls=%async_computation.11 | async-start | bytes 9732096 | tf_op jit(solution)/shard_map/reduce_scatter | solution.py:302
  810.2 590.0 %reduce-scatter.14.cloned.1.call-start = ((), (), s32[]{:S(2)}) async-start(), calls=%async_computation.12 | async-start | bytes 9732096 | tf_op jit(solution)/shard_map/reduce_scatter | solution.py:304
  (110 other events, 444.2 us)
Sparse Core Ops, SparseCore 0:
  10.9 63.3 all-gather.4
  77.2 54.1 all-gather.6
  134.3 62.6 all-gather.8
  199.8 62.3 all-gather.10
  796.1 91.3 reduce-scatter.15
  894.1 98.1 reduce-scatter.9
  998.5 118.0 reduce-scatter.7
  1124.1 134.8 reduce-scatter.11
  1265.5 134.6 reduce-scatter.13
where the time goes:
time: 1410 us
  waiting for transfers between devices  607 us (43%)
  matrix products  467 us (33%)
  other arithmetic  134 us (10%)
  blocking collectives  122 us (9%)
  local copies, waits for them, and re-layouts  55.5 us (4%)
  between operations  15.2 us (1%)
    reduce_scatter x1, waiting for transfers between devices, shards(): lax.psum_scatter(grad_in, ('grp', 'dev'), scatter_dimension=0, tiled=True)  142 us
    reduce_scatter x1, waiting for transfers between devices, shards(): lax.psum_scatter(grad_back, ('grp', 'dev'), scatter_dimension=0, tiled=True)  141 us
    reduce_scatter x1, waiting for transfers between devices, shards(): lax.psum_scatter(grad_qkv, ('grp', 'dev'), scatter_dimension=0, tiled=True)  124 us
    dot_general x8, matrix products, block_scores(): jnp.einsum('kij,kh->hij', kernels_low, pair_weight, preferred_element_typ...  108 us
    dot_general x4, matrix products, backward_block(): jnp.einsum('hij,kh->kij', grad_scores, pair_weight, preferred_element_typ...  107 us
    reduce_scatter x1, waiting for transfers between devices, shards(): lax.psum_scatter(grad_out_weight, ('grp', 'dev'), scatter_dimension=0, ti...  105 us
    reduce_sum x4, other arithmetic, gaussian(): (distance[None] - kern_mean[:, None, None]) / kern_width[:, None, None]  84.9 us
    unnamed x2, blocking collectives  80.3 us
  transfers between devices with their start and end apart: 17, of which 9 were waited for; matrix products, arithmetic and copies ran while one was open for 12% of the time, Pallas kernels for 0%

commit v1 on v0

v1 whole, which is shorter than its diff:
```python
import math

import jax
import jax.numpy as jnp
from jax import lax
from jax.experimental import pallas as pl
from jax.experimental.pallas import tpu as pltpu
from jax.sharding import PartitionSpec as P

D = 768
HEADS = 32
HDIM = 24
KERN = 128
TFREQ = 128
BIN = 1024
GROUPS = 4
GHEADS = HEADS // GROUPS
GWIDTH = GHEADS * HDIM
PAIR_ROWS = 8
ATT_ROWS = 128

norm_eps = 1e-05
mask_fill = -1e30
log2e = math.log2(math.e)
center = 6.0
f32 = jnp.float32
bf16 = jnp.bfloat16
VMEM_LIMIT = 56 * 1024 * 1024


def lanes_dot(left, right):
    return lax.dot_general(left, right, (((1,), (1,)), ((), ())), preferred_element_type=f32)


def dot(left, right):
    return jnp.dot(left, right, preferred_element_type=f32)


def pair_block(places_i, segs_i, places_j, segs_j, coef, weight_t, dist_ref, phi_ref, bias_ref, mask_scr):
    square = None
    for axis in range(3):
        gap = places_i[:, axis : axis + 1] - places_j[axis : axis + 1, :]
        square = gap * gap if square is None else square + gap * gap
    dist_ref[...] = jnp.sqrt(square)
    mask_scr[...] = jnp.where(segs_i == segs_j, 0.0, mask_fill).astype(f32)
    for u in range(PAIR_ROWS):
        for kg in range(KERN // 16):
            rows = slice(kg * 16, kg * 16 + 16)
            mean, inv, shift = coef[0, rows, :], coef[1, rows, :], coef[2, rows, :]
            for jv in range(BIN // 128):
                dist = dist_ref[u : u + 1, jv * 128 : jv * 128 + 128]
                z = (dist - mean) * inv
                lanes = slice(u * BIN + jv * 128, u * BIN + jv * 128 + 128)
                phi_ref[rows, lanes] = jnp.exp2(shift - z * z).astype(bf16)
    bias = dot(weight_t[...], phi_ref[...])
    for u in range(PAIR_ROWS):
        part = bias[:, u * BIN : u * BIN + BIN] * log2e + mask_scr[u : u + 1, :]
        for g in range(GROUPS):
            bias_ref[g, u * GHEADS : u * GHEADS + GHEADS, :] = part[g * GHEADS : g * GHEADS + GHEADS, :]


def pair_kernel(places_i, segs_i, places_j, segs_j, coef, weight_t, dist_ref, phi_ref, bias_ref, mask_scr):
    pair_block(
        places_i[...], segs_i[...], places_j[...], segs_j[...], coef, weight_t, dist_ref, phi_ref.at[0], bias_ref, mask_scr
    )


def pair_call(places_i, segs_i, places_j, segs_j, coef, weight_t):
    rows = places_i.shape[0]
    steps = rows // PAIR_ROWS
    return pl.pallas_call(
        pair_kernel,
        grid=(steps,),
        in_specs=[
            pl.BlockSpec((PAIR_ROWS, 3), lambda i: (i, 0)),
            pl.BlockSpec((PAIR_ROWS, 1), lambda i: (i, 0)),
            pl.BlockSpec((3, BIN), lambda i: (0, 0)),
            pl.BlockSpec((1, BIN), lambda i: (0, 0)),
            pl.BlockSpec((3, KERN, 128), lambda i: (0, 0, 0)),
            pl.BlockSpec((HEADS, KERN), lambda i: (0, 0)),
        ],
        out_specs=[
            pl.BlockSpec((PAIR_ROWS, BIN), lambda i: (i, 0)),
            pl.BlockSpec((1, KERN, PAIR_ROWS * BIN), lambda i: (i, 0, 0)),
            pl.BlockSpec((GROUPS, PAIR_ROWS * GHEADS, BIN), lambda i: (0, i, 0)),
        ],
        out_shape=[
            jax.ShapeDtypeStruct((rows, BIN), f32),
            jax.ShapeDtypeStruct((steps, KERN, PAIR_ROWS * BIN), bf16),
            jax.ShapeDtypeStruct((GROUPS, rows * GHEADS, BIN), f32),
        ],
        scratch_shapes=[pltpu.VMEM((PAIR_ROWS, BIN), f32)],
        compiler_params=pltpu.CompilerParams(vmem_limit_bytes=VMEM_LIMIT),
        name="pair_forward",
    )(places_i, segs_i, places_j, segs_j, coef, weight_t)


def spread_tables():
    rows = ATT_ROWS * GHEADS
    spread = (lax.broadcasted_iota(jnp.int32, (rows, ATT_ROWS), 0) // GHEADS) == lax.broadcasted_iota(
        jnp.int32, (rows, ATT_ROWS), 1
    )
    gather = (lax.broadcasted_iota(jnp.int32, (ATT_ROWS, rows), 1) // GHEADS) == lax.broadcasted_iota(
        jnp.int32, (ATT_ROWS, rows), 0
    )
    head = (lax.broadcasted_iota(jnp.int32, (rows, GWIDTH), 0) % GHEADS) == (
        lax.broadcasted_iota(jnp.int32, (rows, GWIDTH), 1) // HDIM
    )
    head_t = (lax.broadcasted_iota(jnp.int32, (GWIDTH, rows), 1) % GHEADS) == (
        lax.broadcasted_iota(jnp.int32, (GWIDTH, rows), 0) // HDIM
    )
    return spread.astype(bf16), gather.astype(bf16), head.astype(bf16), head_t.astype(bf16)


def forward_kernel(q_ref, k_ref, v_ref, bias_ref, spread, gather, head, head_t, out_ref, prob_ref, s_scr):
    rows = ATT_ROWS * GHEADS
    query = (lanes_dot(spread[...], q_ref[...]).astype(bf16)) * head[...]
    s_scr[...] = dot(query, k_ref[...])
    chunk = 32

    def soft(t, carry):
        at = pl.ds(pl.multiple_of(t * chunk, chunk), chunk)
        score = s_scr[at, :] * (HDIM**-0.5 * log2e) + bias_ref[0, at, :]
        top = jnp.max(score, axis=-1, keepdims=True)
        weight = jnp.exp2(score - top)
        total = jnp.sum(weight, axis=-1, keepdims=True)
        prob_ref[0, at, :] = (weight * (1.0 / total)).astype(bf16)
        return carry

    lax.fori_loop(0, rows // chunk, soft, 0)
    mixed = lanes_dot(v_ref[...], prob_ref[0])
    mixed = mixed.astype(bf16) * head_t[...]
    out_ref[...] = lanes_dot(mixed, gather[...]).astype(bf16)


def forward_call(q_t, k_t, v_t, bias, tables):
    rows = q_t.shape[1]
    blocks = rows // ATT_ROWS
    wide = ATT_ROWS * GHEADS
    whole = lambda g, i: (0, 0)
    return pl.pallas_call(
        forward_kernel,
        grid=(GROUPS, blocks),
        in_specs=[
            pl.BlockSpec((GWIDTH, ATT_ROWS), lambda g, i: (g, i)),
            pl.BlockSpec((GWIDTH, BIN), lambda g, i: (g, 0)),
            pl.BlockSpec((GWIDTH, BIN), lambda g, i: (g, 0)),
            pl.BlockSpec((1, wide, BIN), lambda g, i: (g, i, 0)),
            pl.BlockSpec((wide, ATT_ROWS), whole),
            pl.BlockSpec((ATT_ROWS, wide), whole),
            pl.BlockSpec((wide, GWIDTH), whole),
            pl.BlockSpec((GWIDTH, wide), whole),
        ],
        out_specs=[
            pl.BlockSpec((GWIDTH, ATT_ROWS), lambda g, i: (g, i)),
            pl.BlockSpec((1, wide, BIN), lambda g, i: (g, i, 0)),
        ],
        out_shape=[
            jax.ShapeDtypeStruct((D, rows), bf16),
            jax.ShapeDtypeStruct((GROUPS, rows * GHEADS, BIN), bf16),
        ],
        scratch_shapes=[pltpu.VMEM((wide, BIN), f32)],
        compiler_params=pltpu.CompilerParams(vmem_limit_bytes=VMEM_LIMIT),
        name="attention_forward",
    )(q_t, k_t, v_t, bias, *tables)


def backward_kernel(
    q_ref, go_ref, k_ref, v_ref, prob_ref, spread, gather, head, head_t, gs_ref, gq_ref, gk_ref, gv_ref, s_scr
):
    rows = ATT_ROWS * GHEADS
    step = pl.program_id(1)
    last = pl.num_programs(1) - 1
    grad_out = (lanes_dot(spread[...], go_ref[...]).astype(bf16)) * head[...]
    s_scr[...] = dot(grad_out, v_ref[...])
    chunk = 32

    def soft(t, carry):
        at = pl.ds(pl.multiple_of(t * chunk, chunk), chunk)
        prob = prob_ref[0, at, :].astype(f32)
        grad_prob = s_scr[at, :]
        inner = jnp.sum(prob * grad_prob, axis=-1, keepdims=True)
        gs_ref[0, at, :] = (prob * (grad_prob - inner)).astype(bf16)
        return carry

    lax.fori_loop(0, rows // chunk, soft, 0)
    grad_query = lanes_dot(k_ref[...], gs_ref[0]) * (HDIM**-0.5)
    grad_query = grad_query.astype(bf16) * head_t[...]
    gq_ref[...] = lanes_dot(grad_query, gather[...]).astype(bf16)
    query_t = lanes_dot(q_ref[...], spread[...]).astype(bf16) * head_t[...]
    grad_out_t = lanes_dot(go_ref[...], spread[...]).astype(bf16) * head_t[...]
    grad_key = dot(query_t, gs_ref[0]) * (HDIM**-0.5)
    grad_value = dot(grad_out_t, prob_ref[0])

    @pl.when(step == 0)
    def _():
        gk_ref[...] = grad_key
        gv_ref[...] = grad_value

    @pl.when(step > 0)
    def _():
        gk_ref[...] += grad_key
        gv_ref[...] += grad_value


def backward_call(q_t, go_t, k_t, v_t, prob, tables):
    rows = q_t.shape[1]
    blocks = rows // ATT_ROWS
    wide = ATT_ROWS * GHEADS
    whole = lambda g, i: (0, 0)
    return pl.pallas_call(
        backward_kernel,
        grid=(GROUPS, blocks),
        in_specs=[
            pl.BlockSpec((GWIDTH, ATT_ROWS), lambda g, i: (g, i)),
            pl.BlockSpec((GWIDTH, ATT_ROWS), lambda g, i: (g, i)),
            pl.BlockSpec((GWIDTH, BIN), lambda g, i: (g, 0)),
            pl.BlockSpec((GWIDTH, BIN), lambda g, i: (g, 0)),
            pl.BlockSpec((1, wide, BIN), lambda g, i: (g, i, 0)),
            pl.BlockSpec((wide, ATT_ROWS), whole),
            pl.BlockSpec((ATT_ROWS, wide), whole),
            pl.BlockSpec((wide, GWIDTH), whole),
            pl.BlockSpec((GWIDTH, wide), whole),
        ],
        out_specs=[
            pl.BlockSpec((1, wide, BIN), lambda g, i: (g, i, 0)),
            pl.BlockSpec((GWIDTH, ATT_ROWS), lambda g, i: (g, i)),
            pl.BlockSpec((GWIDTH, BIN), lambda g, i: (g, 0)),
            pl.BlockSpec((GWIDTH, BIN), lambda g, i: (g, 0)),
        ],
        out_shape=[
            jax.ShapeDtypeStruct((GROUPS, rows * GHEADS, BIN), bf16),
            jax.ShapeDtypeStruct((D, rows), bf16),
            jax.ShapeDtypeStruct((D, BIN), f32),
            jax.ShapeDtypeStruct((D, BIN), f32),
        ],
        scratch_shapes=[pltpu.VMEM((wide, BIN), f32)],
        compiler_params=pltpu.CompilerParams(vmem_limit_bytes=VMEM_LIMIT),
        name="attention_backward",
    )(q_t, go_t, k_t, v_t, prob, *tables)


def pair_grad_kernel(gs_ref, dist_ref, phi_ref, sum_ref, terms):
    @pl.when(pl.program_id(0) == 0)
    def _():
        sum_ref[...] = jnp.zeros_like(sum_ref)

    for u in range(PAIR_ROWS):
        lanes = slice(u * BIN, u * BIN + BIN)
        dist = dist_ref[u : u + 1, :] - center
        for g in range(0, GROUPS, 2):
            low = gs_ref[g, u * GHEADS : u * GHEADS + GHEADS, :].astype(f32)
            high = gs_ref[g + 1, u * GHEADS : u * GHEADS + GHEADS, :].astype(f32)
            grad = jnp.concatenate([low, high], axis=0)
            once = grad * dist
            twice = once * dist
            once_top = once.astype(bf16)
            twice_top = twice.astype(bf16)
            pieces = (
                grad.astype(bf16),
                once_top,
                (once - once_top.astype(f32)).astype(bf16),
                twice_top,
                (twice - twice_top.astype(f32)).astype(bf16),
            )
            for at, piece in enumerate(pieces):
                terms[at * HEADS + g * GHEADS : at * HEADS + (g + 2) * GHEADS, lanes] = piece
    sum_ref[...] += lanes_dot(terms[...], phi_ref[0])


def pair_grad_call(gs, dist, phi):
    rows = dist.shape[0]
    steps = rows // PAIR_ROWS
    return pl.pallas_call(
        pair_grad_kernel,
        grid=(steps,),
        in_specs=[
            pl.BlockSpec((GROUPS, PAIR_ROWS * GHEADS, BIN), lambda i: (0, i, 0)),
            pl.BlockSpec((PAIR_ROWS, BIN), lambda i: (i, 0)),
            pl.BlockSpec((1, KERN, PAIR_ROWS * BIN), lambda i: (i, 0, 0)),
        ],
        out_specs=pl.BlockSpec((5 * HEADS, KERN), lambda i: (0, 0)),
        out_shape=jax.ShapeDtypeStruct((5 * HEADS, KERN), f32),
        scratch_shapes=[pltpu.VMEM((5 * HEADS, PAIR_ROWS * BIN), bf16)],
        compiler_params=pltpu.CompilerParams(vmem_limit_bytes=VMEM_LIMIT),
        name="pair_gradient",
    )(gs, dist, phi)


def layer_norm(values, norm_gain, norm_offset):
    middle = values - jnp.mean(values, axis=-1, keepdims=True)
    spread = jnp.mean(middle * middle, axis=-1, keepdims=True)
    return middle * lax.rsqrt(spread + norm_eps) * norm_gain + norm_offset


def time_features(time_values):
    half_count = TFREQ // 2
    frequency = jnp.exp(jnp.arange(half_count, dtype=f32) * (-math.log(10000.0) / half_count))
    angles = (1000.0 * time_values)[:, None] * frequency[None, :]
    return jnp.concatenate([jnp.sin(angles), jnp.cos(angles)], axis=1)


def from_partner(block, bit):
    count = lax.axis_size("dev")
    return lax.ppermute(block, "dev", [(at, at ^ bit) for at in range(count)])


def of_block(own):
    across = from_partner(own, 2)
    beside = from_partner(own, 1)
    diagonal = from_partner(across, 1)
    return own, beside, across, diagonal


def outer_sum(left_rows, right_rows):
    return lax.dot_general(left_rows, right_rows, (((0,), (0,)), ((), ())), preferred_element_type=f32)


def times_transposed(left_rows, weight_matrix):
    return lax.dot_general(left_rows, weight_matrix, (((1,), (1,)), ((), ())), preferred_element_type=f32)


def shards(
    atoms,
    positions,
    segment,
    item_time,
    time_weight,
    norm1_gain,
    norm1_bias,
    qkv_weight,
    out_weight,
    norm2_gain,
    norm2_bias,
    ffn_in,
    ffn_in_bias,
    ffn_out,
    ffn_out_bias,
    pair_weight,
    kernel_mean,
    kernel_width,
    cotangent,
):
    axes = ("grp", "dev")
    gather = lambda array, axis: lax.all_gather(array, axes, axis=axis, tiled=True)
    w_time = gather(time_weight, 1)
    gain_one, shift_one = gather(norm1_gain, 0).astype(f32), gather(norm1_bias, 0).astype(f32)
    w_qkv = gather(qkv_weight, 0)
    w_out = gather(out_weight, 0)
    gain_two, shift_two = gather(norm2_gain, 0).astype(f32), gather(norm2_bias, 0).astype(f32)
    w_in = gather(ffn_in, 0)
    bias_in = gather(ffn_in_bias, 0).astype(f32)
    w_back = gather(ffn_out, 0)
    bias_back = gather(ffn_out_bias, 0).astype(f32)

    places = jnp.concatenate([positions, segment.astype(f32)[None]], axis=0)
    places_all = jnp.concatenate(of_block(places), axis=1)
    places_i = places.T
    column = lambda values: jnp.broadcast_to(values[:, None], (KERN, 128))
    coef = jnp.stack(
        [
            column(kernel_mean),
            column(math.sqrt(0.5 * log2e) / kernel_width),
            column(-jnp.log2(math.sqrt(2.0 * math.pi) * kernel_width)),
        ]
    )
    dist, phi, bias = pair_call(places_i[:, :3], places_i[:, 3:], places_all[:3], places_all[3:], coef, pair_weight.T)
    tables = spread_tables()

    features = time_features(item_time).astype(bf16)
    stream_zero = atoms.astype(f32) + dot(features, w_time)
    normed = layer_norm(stream_zero, gain_one, shift_one).astype(bf16)
    packed_t = lax.dot_general(w_qkv, normed, (((0,), (1,)), ((), ())), preferred_element_type=f32).astype(bf16)
    q_t = packed_t[:D]
    kv_t = jnp.concatenate(of_block(packed_t[D:]), axis=1)
    k_t, v_t = kv_t[:D], kv_t[D:]
    mixed_t, prob = forward_call(q_t, k_t, v_t, bias, tables)

    stream_one = stream_zero + lax.dot_general(mixed_t, w_out, (((0,), (0,)), ((), ())), preferred_element_type=f32)
    second = layer_norm(stream_one, gain_two, shift_two).astype(bf16)
    hidden_pre = dot(second, w_in) + bias_in
    hidden_act = jax.nn.gelu(hidden_pre, approximate=False).astype(bf16)
    output = (stream_one + dot(hidden_act, w_back) + bias_back).astype(bf16)

    grad_output = cotangent.astype(f32)
    grad_branch = cotangent
    grad_back = outer_sum(hidden_act, grad_branch)
    grad_bias_back = jnp.sum(grad_output, axis=0)
    grad_act = times_transposed(grad_branch, w_back)
    _, gelu_pull = jax.vjp(lambda pre: jax.nn.gelu(pre, approximate=False), hidden_pre)
    grad_pre = gelu_pull(grad_act)[0].astype(bf16)
    grad_in = outer_sum(second, grad_pre)
    grad_bias_in = jnp.sum(grad_pre.astype(f32), axis=0)
    grad_second = times_transposed(grad_pre, w_in)
    _, norm_two_pull = jax.vjp(layer_norm, stream_one, gain_two, shift_two)
    grad_stream_part, grad_gain_two, grad_shift_two = norm_two_pull(grad_second)
    grad_stream_one = grad_output + grad_stream_part
    grad_attn = grad_stream_one.astype(bf16)
    grad_out_weight = dot(mixed_t, grad_attn)
    grad_mixed_t = times_transposed(w_out, grad_attn).astype(bf16)

    gs, grad_query_t, grad_key_t, grad_value_t = backward_call(q_t, grad_mixed_t, k_t, v_t, prob, tables)
    sums = pair_grad_call(gs, dist, phi)

    rows = atoms.shape[0]
    grad_kv = jnp.concatenate([grad_key_t, grad_value_t], axis=0)
    part = [grad_kv[:, at * rows : at * rows + rows] for at in range(BIN // rows)]
    own = part[0] + from_partner(part[1].astype(bf16), 1).astype(f32)
    far = part[2] + from_partner(part[3].astype(bf16), 1).astype(f32)
    own = own + from_partner(far.astype(bf16), 2).astype(f32)
    grad_packed_t = jnp.concatenate([grad_query_t, own.astype(bf16)], axis=0)
    grad_qkv = lax.dot_general(normed, grad_packed_t, (((0,), (1,)), ((), ())), preferred_element_type=f32)
    grad_normed = lax.dot_general(grad_packed_t, w_qkv, (((0,), (1,)), ((), ())), preferred_element_type=f32)
    _, norm_one_pull = jax.vjp(layer_norm, stream_zero, gain_one, shift_one)
    grad_zero_part, grad_gain_one, grad_shift_one = norm_one_pull(grad_normed)
    grad_input = grad_stream_one + grad_zero_part
    grad_time = outer_sum(features, grad_input.astype(bf16))

    scatter = lambda array, axis: lax.psum_scatter(array, axes, scatter_dimension=axis, tiled=True)
    sums = lax.psum(sums, axes)
    weight_t = pair_weight.astype(f32).T
    low = sums[:HEADS]
    once = sums[HEADS : 2 * HEADS] + sums[2 * HEADS : 3 * HEADS]
    twice = sums[3 * HEADS : 4 * HEADS] + sums[4 * HEADS :]
    zeroth, first, square = (jnp.sum(weight_t * part_sum, axis=0) for part_sum in (low, once, twice))
    mean = kernel_mean - center
    grad_mean = (first - mean * zeroth) / (kernel_width * kernel_width)
    grad_width = (square - 2.0 * mean * first + mean * mean * zeroth) / (
        kernel_width * kernel_width * kernel_width
    ) - zeroth / kernel_width
    return (
        output,
        grad_input,
        scatter(grad_time, 1),
        scatter(grad_gain_one, 0),
        scatter(grad_shift_one, 0),
        scatter(grad_qkv, 0),
        scatter(grad_out_weight, 0),
        scatter(grad_gain_two, 0),
        scatter(grad_shift_two, 0),
        scatter(grad_in, 0),
        scatter(grad_bias_in, 0),
        scatter(grad_back, 0),
        scatter(grad_bias_back, 0),
        low.T,
        grad_mean,
        grad_width,
    )


def solution(mesh):
    in_specs = (
        P(("grp", "dev"), None),
        P(None, ("grp", "dev")),
        P(("grp", "dev")),
        P(("grp", "dev")),
        P(None, ("grp", "dev")),
        P(("grp", "dev")),
        P(("grp", "dev")),
        P(("grp", "dev"), None),
        P(("grp", "dev"), None),
        P(("grp", "dev")),
        P(("grp", "dev")),
        P(("grp", "dev"), None),
        P(("grp", "dev")),
        P(("grp", "dev"), None),
        P(("grp", "dev")),
        P(),
        P(),
        P(),
        P(("grp", "dev"), None),
    )
    out_specs = (
        P(("grp", "dev"), None),
        P(("grp", "dev"), None),
        P(None, ("grp", "dev")),
        P(("grp", "dev")),
        P(("grp", "dev")),
        P(("grp", "dev"), None),
        P(("grp", "dev"), None),
        P(("grp", "dev")),
        P(("grp", "dev")),
        P(("grp", "dev"), None),
        P(("grp", "dev")),
        P(("grp", "dev"), None),
        P(("grp", "dev")),
        P(),
        P(),
        P(),
    )
    return jax.shard_map(shards, mesh=mesh, in_specs=in_specs, out_specs=out_specs, check_vma=False)
```

time: 1410 us -> 1150 us (0.82)
  matrix products: 467 us -> 53 us
  Pallas kernels: 0 us -> 227 us
  other arithmetic: 134 us -> 29.9 us
  waiting for transfers between devices: 607 us -> 671 us
  local copies, waits for them, and re-layouts: 55.5 us -> 23.2 us
    dot_general x58 -> x14, matrix products: 467 us -> 53 us  [the longest x3 15.6 us: times_transposed(): lax.dot_general(left_rows, weight_matrix, (((1,), (1,)), ((), ())), prefe...]
    pallas_call x0 -> x4, Pallas kernels: none -> 227 us  [the longest x1 70.9 us: forward_call(): pl.pallas_call(forward_kernel, grid=(GROUPS, blocks), in_specs=[pl.BlockS...]
    reduce_sum x21 -> x6, other arithmetic: 93.3 us -> 3.38 us  [the longest x1 1.4 us: shards(): jnp.sum(weight_t * part_sum, axis=0)]
    psum x0 -> x1, waiting for transfers between devices: none -> 81 us  [shards(): sums = lax.psum(sums, axes)]
    ppermute x8 -> x9, waiting for transfers between devices: 70.2 us -> 21 us  [from_partner(): return lax.ppermute(block, 'dev', [(at, at ^ bit) for at in range(count)])]
    unnamed x10 -> x11, waiting for transfers between devices: 24.2 us -> 56.7 us
  transfers between devices with their start and end apart: 17 -> 19, of which waited for: 9 -> 8; matrix products, arithmetic and copies ran while one was open for 12% -> 7% of each run, Pallas kernels for 0% -> 15%
where the time goes in v1:
time: 1150 us
  waiting for transfers between devices  671 us (58%)
  Pallas kernels  227 us (20%)
  blocking collectives  126 us (11%)
  matrix products  53 us (5%)
  other arithmetic  29.9 us (3%)
  local copies, waits for them, and re-layouts  23.2 us (2%)
  between operations  14.8 us (1%)
    reduce_scatter x4, waiting for transfers between devices, shards(): lax.psum_scatter(array, axes, scatter_dimension=axis, tiled=True)  513 us
    unnamed x2, blocking collectives  82.7 us
    psum x1, waiting for transfers between devices, shards(): sums = lax.psum(sums, axes)  81 us
    pallas_call x1, Pallas kernels, forward_call(): pl.pallas_call(forward_kernel, grid=(GROUPS, blocks), in_specs=[pl.BlockS...  70.9 us
    pallas_call x1, Pallas kernels, backward_call(): pl.pallas_call(backward_kernel, grid=(GROUPS, blocks), in_specs=[pl.Block...  57 us
    unnamed x11, waiting for transfers between devices  56.7 us
    pallas_call x1, Pallas kernels, pair_call(): pl.pallas_call(pair_kernel, grid=(steps,), in_specs=[pl.BlockSpec((PAIR_R...  53.8 us
    pallas_call x1, Pallas kernels, pair_grad_call(): pl.pallas_call(pair_grad_kernel, grid=(steps,), in_specs=[pl.BlockSpec((G...  45.8 us
  transfers between devices with their start and end apart: 19, of which 8 were waited for; matrix products, arithmetic and copies ran while one was open for 7% of the time, Pallas kernels for 15%

profile of v1, /device:TPU:0, one launch (start us, length us, event | category | flops | bytes accessed | tf_op | source)
XLA Modules:
  0.0 1150.5 jit_solution(9942612487780259947)
XLA Ops:
  11.3 1.3 pad_maximum_fusion.10
  12.6 2.9 collective-permute-start.4
  20.5 40.1 %all-reduce.14 = (bf16[768]{0:T(1024)(128)(2,1)S(1)}, bf16[768]{0:T(1024)(128)(2,1)S(1)}, bf16[3072]{0:T(1024)(128)(2,1)}, bf16[768]{0:T(1024)(128)(2,1)}, bf16[...) all-reduce(bf16[768]{0:T(1024)(128)(2,1)S(1)} %dynamic-update-slice.1, ...), channel_id=1, replica_groups=mesh['grp'=4,'dev'=8] {'grp','dev'}, use_global_device_ids=true, to_apply=%add.1 | all-reduce | flops 6912 | bytes 27648
  60.6 42.8 %all_gather.33 = bf16[128,768]{0,1:T(8,128)(2,1)S(1)} all-gather(bf16[128,24]{0,1:T(8,128)(2,1)} %param.23), channel_id=1, replica_groups=mesh['grp'=4,'dev'=8] {'grp','dev'}, dimensions={1}, use_global_device_ids=true | all-gather | bytes 202752 | tf_op jit(solution)/shard_map/all_gather | solution.py:345
  107.4 1.4 fusion.47
  109.7 3.6 fusion
  113.5 1.7 fusion.17.spread
  116.0 0.9 fusion.14.head_t
  117.2 18.1 %collective-permute-done.1 = bf16[1536,256]{1,0:T(8,128)(2,1)S(1)} collective-permute-done((bf16[1536,256]{1,0:T(8,128)(2,1)S(1)}, bf16[1536,256]{1,0:T(8,128)(2,1)S(1)}, u32[]{:S(2)}, u32[]{:S(2)}) %collective-permute-start.1) | collective-permute-done | bytes 786464 | tf_op jit(solution)/shard_map/ppermute | solution.py:305
  135.4 1.6 fusion.13.head
  140.0 1.3 convert_element_type.115
  142.7 1.3 pad_maximum_fusion.9.segs_j
  144.0 1.3 pad_maximum_fusion.8
  145.3 53.8 %pair_forward.1 = (f32[256,1024]{1,0:T(8,128)}, bf16[32,128,8192]{2,1,0:T(8,128)(2,1)}, f32[4,2048,1024]{2,1,0:T(8,128)}) custom-call(f32[256,3]{1,0:T(8,128)} %copy.44.places_i, f32[256,1]{1,0:T(8,128)} %copy.45.segs_i, f32[3,1024]{1,0:T(4,128)} %bitcast.34, f32[1,1024]{1,0:T(1,128)} %pad_maximum_fusion.9.segs_j, f32[3,128,128]{2,1,0:T(8,128)} %pad_maximum_fusion.4.coef, ...), custom_call_target="tpu_custom_call" | custom-call | tf_op jit(solution)/shard_map/pair_forward/pallas_call | solution.py:71
  199.9 1.6 pad_maximum_fusion
  201.5 1.9 fusion.46
  203.4 70.9 %attention_forward.1 = (bf16[768,256]{1,0:T(8,128)(2,1)}, bf16[4,2048,1024]{2,1,0:T(8,128)(2,1)}) custom-call(bf16[768,256]{1,0:T(8,128)(2,1)} %slice.70.q_ref, bf16[768,1024]{1,0:T(8,128)(2,1)} %get-tuple-element.65.k_ref, bf16[768,1024]{1,0:T(8,128)(2,1)} %get-tuple-element.64.v_ref, f32[4,2048,1024]{2,1,0:T(8,128)} %get-tuple-element.25.bias_ref, ...), custom_call_target="tpu_custom_call" | custom-call | tf_op jit(solution)/shard_map/attention_forward/pallas_call | solution.py:141
  274.4 2.0 fusion.48
  276.7 5.5 convolution_add_fusion
  282.2 12.2 %convert_reduce_fusion = (f32[3072]{0:T(1024)}, bf16[256,3072]{1,0:T(8,128)(2,1)S(1)}, f32[256,3072]{1,0:T(8,128)}) fusion(f32[256,3072]{1,0:T(8,128)} %convolution_add_fusion, bf16[256,768]{1,0:T(8,128)(2,1)S(1)} %copy-done.2, bf16[3072,768]{1,0:T(8,128)(2,1)} %all-gather.11.cloned.1.call-done), kind=kOutput, calls=%fused_computation.6 | convolution fusion | flops 1266152448 | bytes 12988416 | tf_op jit(solution)/shard_map/dot_general | solution.py:320
  294.4 2.1 multiply_reduce_fusion
  297.8 1.3 fusion.12.go_ref
  299.1 57.0 %attention_backward.1 = (bf16[4,2048,1024]{2,1,0:T(8,128)(2,1)}, bf16[768,256]{1,0:T(8,128)(2,1)}, f32[768,1024]{1,0:T(8,128)}, f32[768,1024]{1,0:T(8,128)}) custom-call(bf16[768,256]{1,0:T(8,128)(2,1)} %slice.70.q_ref, bf16[768,256]{1,0:T(8,128)(2,1)} %fusion.12.go_ref, bf16[768,1024]{1,0:T(8,128)(2,1)} %get-tuple-element.65.k_ref, ...), custom_call_target="tpu_custom_call" | custom-call | tf_op jit(solution)/shard_map/attention_backward/pallas_call | solution.py:211
  356.2 2.3 constant_dynamic-update-slice_fusion.1
  359.7 1.4 fusion.45
  361.7 2.9 collective-permute-done.7
  364.5 1.2 fusion.7
  365.9 45.8 %pair_gradient.1 = f32[160,128]{1,0:T(8,128)} custom-call(bf16[4,2048,1024]{2,1,0:T(8,128)(2,1)} %get-tuple-element.31.gs_ref, f32[256,1024]{1,0:T(8,128)} %get-tuple-element.32.dist_ref, bf16[32,128,8192]{2,1,0:T(8,128)(2,1)} %get-tuple-element.33.phi_ref), custom_call_target="tpu_custom_call" | custom-call | tf_op jit(solution)/shard_map/pair_gradient/pallas_call | solution.py:274
  411.8 2.2 fusion.9
  414.8 1.9 multiply_reduce_fusion.1
  417.0 0.9 convert_reduce_fusion.1
  417.9 0.9 copy-done.4
  418.8 1.1 fusion.20
  419.9 1.9 fusion.49
  422.2 5.3 fusion.15
  427.6 1.3 copy-done.9
  428.9 5.2 fusion.41
  434.2 3.4 multiply_convert_fusion
  437.6 5.1 fusion.50
  443.4 4.5 fusion.11
  447.9 81.0 %all-reduce.17.cloned.1.call-done = f32[160,128]{1,0:T(8,128)} async-done(((f32[160,128]{1,0:T(8,128)}), f32[160,128]{1,0:T(8,128)}) %all-reduce.17.cloned.1.call-update) | async-done | bytes 81936 | tf_op jit(solution)/shard_map/psum | solution.py:420
  528.9 1.4 fusion.26
  530.9 42.7 %all-reduce.13 = (f32[768]{0:T(1024)S(1)}, f32[768]{0:T(1024)S(1)}, f32[768]{0:T(1024)S(1)}, f32[768]{0:T(1024)S(1)}, f32[3072]{0:T(1024)S(1)}, /*index=5*/f32[768]{0:T(1024)S(1)}) all-reduce(f32[768]{0:T(1024)S(1)} %copy-done.43, f32[768]{0:T(1024)S(1)} %copy-done.44, ...), channel_id=3, replica_groups=mesh['grp'=4,'dev'=8] {'grp','dev'}, use_global_device_ids=true, to_apply=%region_10.11.clone | all-reduce | flops 6912 | bytes 55296
  577.1 54.0 %reduce-scatter.16.cloned.1.call-done = f32[128,24]{0,1:T(8,128)} async-done(((f32[128,768]{0,1:T(8,128)}), f32[128,24]{0,1:T(8,128)}) %reduce-scatter.16.cloned.1.call-update) | async-done | bytes 12304
  631.1 104.9 %reduce-scatter.10.cloned.1.call-done = f32[24,768]{1,0:T(8,128)} async-done(((f32[768,768]{1,0:T(8,128)}), f32[24,768]{1,0:T(8,128)}) %reduce-scatter.10.cloned.1.call-update) | async-done | bytes 73744 | tf_op jit(solution)/shard_map/reduce_scatter | solution.py:419
  736.0 124.3 %reduce-scatter.8.cloned.1.call-done = f32[24,2304]{1,0:T(8,128)} async-done(((f32[768,2304]{1,0:T(8,128)}), f32[24,2304]{1,0:T(8,128)}) %reduce-scatter.8.cloned.1.call-update) | async-done | bytes 221200 | tf_op jit(solution)/shard_map/reduce_scatter | solution.py:419
  860.3 142.4 %reduce-scatter.12.cloned.1.call-done = f32[24,3072]{1,0:T(8,128)} async-done(((f32[768,3072]{1,0:T(8,128)}), f32[24,3072]{1,0:T(8,128)}) %reduce-scatter.12.cloned.1.call-update) | async-done | bytes 294928 | tf_op jit(solution)/shard_map/reduce_scatter | solution.py:419
  1002.7 140.9 %reduce-scatter.14.cloned.1.call-done = f32[96,768]{1,0:T(8,128)} async-done(((f32[3072,768]{1,0:T(8,128)}), f32[96,768]{1,0:T(8,128)}) %reduce-scatter.14.cloned.1.call-update) | async-done | bytes 294928 | tf_op jit(solution)/shard_map/reduce_scatter | solution.py:419
  (202 shorter events, 30.2 us)
Async XLA Ops:
  7.2 101.9 %all-gather.5.cloned.1.call-start = ((), (), s32[]{:S(2)}) async-start(), calls=%async_computation.5 | async-start | bytes 3649536 | tf_op jit(solution)/shard_map/all_gather | solution.py:345
  7.9 266.5 %all-gather.7.cloned.1.call-start = ((), (), s32[]{:S(2)}) async-start(), calls=%async_computation.6 | async-start | bytes 1216512 | tf_op jit(solution)/shard_map/all_gather | solution.py:345
  8.7 268.0 %all-gather.9.cloned.1.call-start = ((), (), s32[]{:S(2)}) async-start(), calls=%async_computation.7 | async-start | bytes 4866048 | tf_op jit(solution)/shard_map/all_gather | solution.py:345
  9.4 272.8 %all-gather.11.cloned.1.call-start = ((), (), s32[]{:S(2)}) async-start(), calls=%async_computation.8 | async-start | bytes 4866048 | tf_op jit(solution)/shard_map/all_gather | solution.py:345
  10.0 519.0 %all-reduce.17.cloned.1.call-start = ((), (), s32[]{:S(2)}) async-start(), calls=%async_computation.13 | async-start | bytes 163840 | tf_op jit(solution)/shard_map/psum | solution.py:420
  12.6 125.3 %collective-permute-start.4 = (f32[4,256]{1,0:T(4,128)}, f32[4,256]{1,0:T(4,128)}, u32[]{:S(2)}, u32[]{:S(2)}) collective-permute-start(f32[4,256]{1,0:T(4,128)} %pad_maximum_fusion.10), channel_id=1, source_target_pairs={{0,2},{1,3},{2,0},{3,1},{4,6},{5,7},{6,4},{7,5},{8,10},{9,11},{10,... | collective-permute-start | bytes 12296 | tf_op jit(solution)/shard_map/ppermute | solution.py:305
  15.5 127.2 %collective-permute-start.3 = (f32[4,256]{1,0:T(4,128)}, f32[4,256]{1,0:T(4,128)}, u32[]{:S(2)}, u32[]{:S(2)}) collective-permute-start(f32[4,256]{1,0:T(4,128)} %pad_maximum_fusion.10), channel_id=1, source_target_pairs={{0,1},{1,0},{2,3},{3,2},{4,5},{5,4},{6,7},{7,6},{8,9},{9,8},{10,11... | collective-permute-start | bytes 12296 | tf_op jit(solution)/shard_map/ppermute | solution.py:305
  109.6 3.9 copy-start.17
  109.6 3.9 copy-start.18
  109.6 3.9 copy-start.40
  109.6 6.4 copy-start.16
  109.6 6.4 copy-start.33
  109.6 6.4 copy-start.34
  109.6 6.3 copy-start.39
  109.7 25.7 %copy-start.48 = (f32[128]{0:T(128)S(1)}, f32[128]{0:T(128)}, u32[]{:S(2)}) copy-start(f32[128]{0:T(128)} %param.36) | copy-start | bytes 1540
  113.3 23.8 %copy-start.45 = (f32[128]{0:T(128)S(1)}, f32[128]{0:T(128)}, u32[]{:S(2)}) copy-start(f32[128]{0:T(128)} %param.35) | copy-start | bytes 1540
  113.3 25.1 %copy-start.15 = (f32[3,256]{1,0:T(4,128)S(1)}, f32[3,256]{1,0:T(4,128)}, u32[]{:S(2)}) copy-start(f32[3,256]{1,0:T(4,128)} %param.20) | copy-start | bytes 9220
  113.3 25.1 %copy-start.21 = (f32[256]{0:T(256)S(1)}, f32[256]{0:T(256)}, u32[]{:S(2)}) copy-start(f32[256]{0:T(256)} %copy-done.20) | copy-start | bytes 3076
  113.4 22.0 %collective-permute-start.1 = (bf16[1536,256]{1,0:T(8,128)(2,1)S(1)}, bf16[1536,256]{1,0:T(8,128)(2,1)S(1)}, u32[]{:S(2)}, u32[]{:S(2)}) collective-permute-start(bf16[1536,256]{1,0:T(8,128)(2,1)S(1)} %slice.71), channel_id=1, source_target_pairs={{0,2},{1,3},{2,0},{3,1},{4,6},{5,7},{6,4},{7,5},{8,10},{9,11},{10,... | collective-permute-start | bytes 2359304 | tf_op jit(solution)/shard_map/ppermute | solution.py:305
  116.9 83.0 %collective-permute-start = (bf16[1536,256]{1,0:T(8,128)(2,1)S(1)}, bf16[1536,256]{1,0:T(8,128)(2,1)}, u32[]{:S(2)}, u32[]{:S(2)}) collective-permute-start(bf16[1536,256]{1,0:T(8,128)(2,1)S(1)} %slice.71), channel_id=1, source_target_pairs={{0,1},{1,0},{2,3},{3,2},{4,5},{5,4},{6,7},{7,6},{8,9},{9,8},{10,11... | collective-permute-start | bytes 2359304 | tf_op jit(solution)/shard_map/ppermute | solution.py:305
  135.4 64.5 %collective-permute-start.2 = (bf16[1536,256]{1,0:T(8,128)(2,1)S(1)}, bf16[1536,256]{1,0:T(8,128)(2,1)}, u32[]{:S(2)}, u32[]{:S(2)}) collective-permute-start(bf16[1536,256]{1,0:T(8,128)(2,1)S(1)} %collective-permute-done.1), channel_id=1, source_target_pairs={{0,1},{1,0},{2,3},{3,2},{4,5},{5,4},{6,7},{7,6},{8,9},{9,8},{10,11... | collective-permute-start | bytes 2359304 | tf_op jit(solution)/shard_map/ppermute | solution.py:305
  137.9 4.8 collective-permute-start.5
  276.4 20.2 %copy-start.24 = (f32[256]{0:T(256)}, f32[256]{0:T(256)S(1)}, u32[]{:S(2)}) copy-start(f32[256]{0:T(256)S(1)} %broadcast_multiply_fusion) | copy-start | bytes 3076
  276.6 20.0 %copy-start.29 = (f32[256]{0:T(256)}, f32[256]{0:T(256)S(1)}, u32[]{:S(2)}) copy-start(f32[256]{0:T(256)S(1)} %fusion.34) | copy-start | bytes 3076
  276.6 5.6 copy-start.2
  282.2 12.2 %copy-start.50 = (bf16[768,3072]{1,0:T(8,128)(2,1)S(1)}, bf16[768,3072]{1,0:T(8,128)(2,1)}, u32[]{:S(2)}) copy-start(bf16[768,3072]{1,0:T(8,128)(2,1)} %all-gather.9.cloned.1.call-done) | copy-start | bytes 14155780
  296.9 59.2 %copy-start.37 = (f32[256]{0:T(256)}, f32[256]{0:T(256)S(1)}, u32[]{:S(2)}) copy-start(f32[256]{0:T(256)S(1)} %negate_multiply_fusion.2) | copy-start | bytes 3076
  356.2 2.8 copy-start.3
  359.2 5.3 copy-start
  361.2 3.4 collective-permute-start.7
  361.2 50.6 %collective-permute-start.6 = (bf16[1536,256]{1,0:T(8,128)(2,1)}, bf16[1536,256]{1,0:T(8,128)(2,1)}, u32[]{:S(2)}, u32[]{:S(2)}) collective-permute-start(bf16[1536,256]{1,0:T(8,128)(2,1)} %get-tuple-element.62), channel_id=1, source_target_pairs={{0,1},{1,0},{2,3},{3,2},{4,5},{5,4},{6,7},{7,6},{8,9},{9,8},{10,11... | collective-permute-start | bytes 2359304 | tf_op jit(solution)/shard_map/ppermute | solution.py:305
  365.7 46.0 %collective-permute-start.8 = (bf16[1536,256]{1,0:T(8,128)(2,1)}, bf16[1536,256]{1,0:T(8,128)(2,1)}, u32[]{:S(2)}, u32[]{:S(2)}) collective-permute-start(bf16[1536,256]{1,0:T(8,128)(2,1)} %fusion.7), channel_id=1, source_target_pairs={{0,2},{1,3},{2,0},{3,1},{4,6},{5,7},{6,4},{7,5},{8,10},{9,11},{10,... | collective-permute-start | bytes 2359304 | tf_op jit(solution)/shard_map/ppermute | solution.py:305
  411.7 219.4 %reduce-scatter.16.cloned.1.call-start = ((), (), s32[]{:S(2)}) async-start(), calls=%async_computation.14 | async-start | bytes 405504
  411.7 3.0 copy-start.51
  416.7 3.3 copy-start.7
  419.9 316.1 %reduce-scatter.10.cloned.1.call-start = ((), (), s32[]{:S(2)}) async-start(), calls=%async_computation.10 | async-start | bytes 2433024 | tf_op jit(solution)/shard_map/reduce_scatter | solution.py:419
  421.9 438.4 %reduce-scatter.8.cloned.1.call-start = ((), (), s32[]{:S(2)}) async-start(), calls=%async_computation.9 | async-start | bytes 7299072 | tf_op jit(solution)/shard_map/reduce_scatter | solution.py:419
  427.5 575.2 %reduce-scatter.12.cloned.1.call-start = ((), (), s32[]{:S(2)}) async-start(), calls=%async_computation.11 | async-start | bytes 9732096 | tf_op jit(solution)/shard_map/reduce_scatter | solution.py:419
  434.2 709.5 %reduce-scatter.14.cloned.1.call-start = ((), (), s32[]{:S(2)}) async-start(), calls=%async_computation.12 | async-start | bytes 9732096 | tf_op jit(solution)/shard_map/reduce_scatter | solution.py:419
  443.4 85.6 %copy-start.19 = (bf16[128,32]{0,1:T(8,128)(2,1)S(1)}, bf16[128,32]{0,1:T(8,128)(2,1)}, u32[]{:S(2)}) copy-start(bf16[128,32]{0,1:T(8,128)(2,1)} %param.34) | copy-start | bytes 24580
  443.4 87.0 %copy-start.46 = (f32[128]{0:T(128)S(1)}, f32[128]{0:T(128)}, u32[]{:S(2)}) copy-start(f32[128]{0:T(128)} %param.35) | copy-start | bytes 1540
  443.4 87.0 %copy-start.49 = (f32[128]{0:T(128)S(1)}, f32[128]{0:T(128)}, u32[]{:S(2)}) copy-start(f32[128]{0:T(128)} %param.36) | copy-start | bytes 1540
  443.4 87.5 %copy-start.26 = (f32[768]{0:T(1024)S(1)}, f32[768]{0:T(1024)}, u32[]{:S(2)}) copy-start(f32[768]{0:T(1024)} %get-tuple-element.66) | copy-start | bytes 9220
  443.4 87.5 %copy-start.32 = (f32[3072]{0:T(1024)S(1)}, f32[3072]{0:T(1024)}, u32[]{:S(2)}) copy-start(f32[3072]{0:T(1024)} %get-tuple-element.55) | copy-start | bytes 36868
  443.4 87.5 %copy-start.41 = (f32[768]{0:T(1024)S(1)}, f32[768]{0:T(1024)}, u32[]{:S(2)}) copy-start(f32[768]{0:T(1024)} %get-tuple-element.34) | copy-start | bytes 9220
  443.4 87.5 %copy-start.42 = (f32[768]{0:T(1024)S(1)}, f32[768]{0:T(1024)}, u32[]{:S(2)}) copy-start(f32[768]{0:T(1024)} %get-tuple-element.38) | copy-start | bytes 9220
  443.4 87.5 %copy-start.43 = (f32[768]{0:T(1024)S(1)}, f32[768]{0:T(1024)}, u32[]{:S(2)}) copy-start(f32[768]{0:T(1024)} %get-tuple-element.36) | copy-start | bytes 9220
  443.4 87.5 %copy-start.44 = (f32[768]{0:T(1024)S(1)}, f32[768]{0:T(1024)}, u32[]{:S(2)}) copy-start(f32[768]{0:T(1024)} %get-tuple-element.39) | copy-start | bytes 9220
  (23 other events, 37.1 us)
Sparse Core Ops, SparseCore 0:
  10.9 62.6 all-gather.4
  76.5 54.4 all-gather.6
  133.9 62.5 all-gather.8
  199.3 63.8 all-gather.10
  411.8 117.1 all-reduce.16
  534.3 96.7 reduce-scatter.15
  637.8 98.1 reduce-scatter.9
  742.2 118.0 reduce-scatter.7
  867.8 134.8 reduce-scatter.11
  1009.0 134.5 reduce-scatter.13

commit v2 on v1

--- a/solution.py
+++ b/solution.py
@@ -1,3 +1,4 @@
+from functools import partial
 import math
 
 import jax
@@ -287,6 +288,388 @@
     )(gs, dist, phi)
 
 
+def grid_of_mesh(mesh):
+    count = mesh.shape["dev"] // 2
+    wide = 1
+    while wide * wide < count:
+        wide *= 2
+    return mesh.shape["grp"], count // wide, wide, 2
+
+
+def my_place(sizes):
+    _, _, wide, cores = sizes
+    dev = lax.axis_index("dev")
+    return (lax.axis_index("grp"), dev // (wide * cores), lax.rem(dev // cores, wide), lax.rem(dev, cores))
+
+
+def device_at(place, sizes):
+    _, _, wide, cores = sizes
+    return (place[0], (place[1] * wide + place[2]) * cores + place[3])
+
+
+def other_place(place, axis, shift, sizes):
+    moved = list(place)
+    moved[axis] = lax.rem(place[axis] + shift, sizes[axis])
+    return tuple(moved)
+
+
+def partner_list(place, sizes):
+    return [other_place(place, axis, shift, sizes) for axis in range(4) for shift in range(1, sizes[axis])]
+
+
+def meet(place, sizes):
+    barrier = pltpu.get_barrier_semaphore()
+    partners = partner_list(place, sizes)
+    for partner in partners:
+        pl.semaphore_signal(
+            barrier, inc=1, device_id=device_at(partner, sizes), device_id_type=pl.DeviceIdType.MESH
+        )
+    pl.semaphore_wait(barrier, len(partners))
+
+
+class GatherPart:
+    def __init__(self, source, full, lanes, order, at, send_sem, recv_sem, place, sizes):
+        self.source, self.full, self.lanes = source, full, lanes
+        self.order = order
+        self.at = at
+        self.send_sem, self.recv_sem = send_sem, recv_sem
+        self.place, self.sizes = place, sizes
+        self.base = [0]
+        for axis in order:
+            self.base.append(self.base[-1] + sizes[axis] - 1)
+
+    def view(self, stage):
+        done = self.order[:stage]
+        where = tuple(slice(None) if axis in done else self.place[axis] for axis in range(4))
+        return self.full.at[where + (slice(None), self.lanes)]
+
+    def copies(self, stage):
+        axis = self.order[stage]
+        found = []
+        for shift in range(1, self.sizes[axis]):
+            sem = self.base[stage] + shift - 1
+            found.append(
+                pltpu.make_async_remote_copy(
+                    src_ref=self.source.at[:, self.lanes] if stage == 0 else self.view(stage),
+                    dst_ref=self.view(stage),
+                    send_sem=self.send_sem.at[self.at, sem],
+                    recv_sem=self.recv_sem.at[self.at, sem],
+                    device_id=device_at(other_place(self.place, axis, shift, self.sizes), self.sizes),
+                    device_id_type=pl.DeviceIdType.MESH,
+                )
+            )
+        return found
+
+    def start(self, stage):
+        for copy in self.copies(stage):
+            copy.start()
+
+    def arrive(self, stage):
+        for copy in self.copies(stage):
+            copy.wait_recv()
+
+    def finish(self):
+        for stage in range(len(self.order)):
+            for copy in self.copies(stage):
+                copy.wait_send()
+
+
+def gather_plan(shapes):
+    plan = []
+    for at, (rows, lanes) in enumerate(shapes):
+        half = lanes // 256 * 128
+        group = [(at, half, lanes - half, (0, 1, 2, 3))]
+        if half:
+            group.insert(0, (at, 0, half, (0, 2, 1, 3)))
+        plan.append(group)
+    return plan
+
+
+def run_stages(groups, stages=4):
+    for part in groups[0]:
+        part.start(0)
+    for turn in range(len(groups) + stages - 1):
+        if turn + 1 < len(groups):
+            for part in groups[turn + 1]:
+                part.start(0)
+        for stage in range(stages - 1, -1, -1):
+            index = turn - stage
+            if 0 <= index < len(groups):
+                for part in groups[index]:
+                    part.arrive(stage)
+                    if stage + 1 < stages:
+                        part.start(stage + 1)
+    for group in groups:
+        for part in group:
+            part.finish()
+
+
+def gather_kernel(sizes, plan, count, *refs):
+    sources, fulls = refs[:count], refs[count : 2 * count]
+    send_sem, recv_sem, own_sem = refs[2 * count :]
+    place = my_place(sizes)
+    own = []
+    for at in range(count):
+        own.append(pltpu.make_async_copy(sources[at], fulls[at].at[place], own_sem.at[at]))
+        own[at].start()
+    meet(place, sizes)
+    groups, index = [], 0
+    for group in plan:
+        groups.append([])
+        for at, first, lanes, order in group:
+            groups[-1].append(
+                GatherPart(sources[at], fulls[at], pl.ds(first, lanes), order, index, send_sem, recv_sem, place, sizes)
+            )
+            index += 1
+    for copy in own:
+        copy.wait()
+    run_stages(groups)
+
+
+def gather_call(sizes, arrays, collective):
+    count = len(arrays)
+    plan = gather_plan([array.shape for array in arrays])
+    slots = sum(size - 1 for size in sizes)
+    fulls = pl.pallas_call(
+        lambda *refs: gather_kernel(sizes, plan, count, *refs),
+        in_specs=[pl.BlockSpec(memory_space=pl.ANY)] * count,
+        out_specs=[pl.BlockSpec(memory_space=pl.ANY)] * count,
+        out_shape=[jax.ShapeDtypeStruct(sizes + array.shape, array.dtype) for array in arrays],
+        scratch_shapes=[
+            pltpu.SemaphoreType.DMA((sum(map(len, plan)), slots)),
+            pltpu.SemaphoreType.DMA((sum(map(len, plan)), slots)),
+            pltpu.SemaphoreType.DMA((count,)),
+        ],
+        compiler_params=pltpu.CompilerParams(
+            collective_id=collective, has_side_effects=True, vmem_limit_bytes=VMEM_LIMIT
+        ),
+        name="gather_weights",
+    )(*arrays)
+    return [full.reshape((-1,) + full.shape[4:]) for full in fulls]
+
+
+class ScatterPart:
+    def __init__(self, source, result, lanes, order, buffers, at, send_sem, recv_sem, own_sem, place, sizes):
+        self.source, self.result, self.lanes = source, result, lanes
+        self.order, self.place, self.sizes = order, place, sizes
+        self.first, self.slots = buffers[0], buffers[1:]
+        self.at, self.send_sem, self.recv_sem, self.own_sem = at, send_sem, recv_sem, own_sem
+        self.base = [0]
+        for axis in order:
+            self.base.append(self.base[-1] + sizes[axis] - 1)
+
+    def pick(self, stage, index):
+        if stage == 0:
+            where = tuple(index if axis == self.order[0] else slice(None) for axis in range(4))
+            return self.source.at[where + (slice(None), self.lanes)]
+        holder = self.first if stage == 1 else self.slots[stage - 1].at[0]
+        left = [axis for axis in range(4) if axis not in self.order[:stage]]
+        where = tuple(index if axis == self.order[stage] else slice(None) for axis in left)
+        return holder.at[where]
+
+    def own_copy(self):
+        return pltpu.make_async_copy(self.pick(0, self.place[self.order[0]]), self.first, self.own_sem.at[self.at])
+
+    def copies(self, stage):
+        axis = self.order[stage]
+        found = []
+        for shift in range(1, self.sizes[axis]):
+            target = other_place(self.place, axis, shift, self.sizes)
+            sem = self.base[stage] + shift - 1
+            found.append(
+                pltpu.make_async_remote_copy(
+                    src_ref=self.pick(stage, target[axis]),
+                    dst_ref=self.slots[stage].at[shift - 1],
+                    send_sem=self.send_sem.at[self.at, sem],
+                    recv_sem=self.recv_sem.at[self.at, sem],
+                    device_id=device_at(target, self.sizes),
+                    device_id_type=pl.DeviceIdType.MESH,
+                )
+            )
+        return found
+
+    def start(self, stage):
+        if stage == 0:
+            self.own_copy().start()
+        for copy in self.copies(stage):
+            copy.start()
+
+    def arrive(self, stage):
+        if stage == 0:
+            self.own_copy().wait()
+        for copy in self.copies(stage):
+            copy.wait_recv()
+        slots = self.slots[stage]
+        count = self.sizes[self.order[stage]] - 1
+        mine = self.first if stage == 0 else self.pick(stage, self.place[self.order[stage]])
+        lead = slots.shape[1:-2]
+        if not lead:
+            total = mine[...].astype(f32)
+            for slot in range(count):
+                total = total + slots[slot].astype(f32)
+            self.result[:, self.lanes] = total
+            return
+        blocks = math.prod(lead)
+
+        def add(step, carry):
+            where = []
+            for size in reversed(lead):
+                where.insert(0, lax.rem(step, size))
+                step = step // size
+            where = tuple(where)
+            total = mine[where].astype(f32)
+            for slot in range(count):
+                total = total + slots[(slot,) + where].astype(f32)
+            if stage == 0:
+                self.first[where] = total.astype(bf16)
+            else:
+                slots[(0,) + where] = total.astype(bf16)
+            return carry
+
+        lax.fori_loop(0, blocks, add, 0)
+
+    def finish(self):
+        for stage in range(len(self.order)):
+            for copy in self.copies(stage):
+                copy.wait_send()
+
+
+class TotalPart:
+    def __init__(self, source, result, slots, send_sem, recv_sem, place, sizes):
+        self.source, self.result, self.slots = source, result, slots
+        self.order, self.place, self.sizes = (3, 2, 1, 0), place, sizes
+        self.send_sem, self.recv_sem = send_sem, recv_sem
+        self.base = [0]
+        for axis in self.order:
+            self.base.append(self.base[-1] + sizes[axis] - 1)
+
+    def copies(self, stage):
+        axis = self.order[stage]
+        mine = self.slots[stage].at[self.place[axis]]
+        found = []
+        for shift in range(1, self.sizes[axis]):
+            sem = self.base[stage] + shift - 1
+            found.append(
+                pltpu.make_async_remote_copy(
+                    src_ref=mine,
+                    dst_ref=mine,
+                    send_sem=self.send_sem.at[sem],
+                    recv_sem=self.recv_sem.at[sem],
+                    device_id=device_at(other_place(self.place, axis, shift, self.sizes), self.sizes),
+                    device_id_type=pl.DeviceIdType.MESH,
+                )
+            )
+        return found
+
+    def start(self, stage):
+        if stage == 0:
+            self.slots[0][self.place[3]] = self.source[...]
+        for copy in self.copies(stage):
+            copy.start()
+
+    def arrive(self, stage):
+        for copy in self.copies(stage):
+            copy.wait_recv()
+        axis = self.order[stage]
+        total = self.slots[stage][0]
+        for at in range(1, self.sizes[axis]):
+            total = total + self.slots[stage][at]
+        if stage == 3:
+            self.result[...] = total
+        else:
+            self.slots[stage + 1][self.place[self.order[stage + 1]]] = total
+
+    def finish(self):
+        for stage in range(4):
+            for copy in self.copies(stage):
+                copy.wait_send()
+
+
+def scatter_plan(shapes):
+    plan = []
+    for at, (rows, lanes) in enumerate(shapes):
+        half = lanes // 256 * 128
+        plan.append([(at, 0, half, (3, 2, 1, 0)), (at, half, lanes - half, (3, 1, 2, 0))])
+    return plan
+
+
+def scatter_buffers(sizes, plan, shapes):
+    buffers = []
+    for at, first, lanes, order in sum(plan, []):
+        block = (shapes[at][0], lanes)
+        left = [0, 1, 2, 3]
+        for stage, axis in enumerate(order):
+            left.remove(axis)
+            lead = tuple(sizes[other] for other in left)
+            if stage == 0:
+                buffers.append(pltpu.VMEM(lead + block, bf16))
+            buffers.append(pltpu.VMEM((sizes[axis] - 1,) + lead + block, bf16))
+    return buffers
+
+
+def scatter_kernel(sizes, plan, count, total_at, *refs):
+    extra = 0 if total_at is None else 1
+    sources, refs = refs[: count + extra], refs[count + extra :]
+    results, refs = refs[: count + extra], refs[count + extra :]
+    send_sem, recv_sem, own_sem = refs[:3]
+    buffers = refs[3:]
+    place = my_place(sizes)
+    meet(place, sizes)
+    groups, index = [], 0
+    for group in plan:
+        groups.append([])
+        for at, first, lanes, order in group:
+            held = buffers[5 * index : 5 * index + 5]
+            lanes = pl.ds(first, lanes)
+            groups[-1].append(
+                ScatterPart(
+                    sources[at], results[at], lanes, order, held, index, send_sem, recv_sem, own_sem, place, sizes
+                )
+            )
+            index += 1
+    if extra:
+        slots = buffers[5 * index : 5 * index + 4]
+        groups[total_at].insert(
+            0, TotalPart(sources[count], results[count], slots, buffers[-2], buffers[-1], place, sizes)
+        )
+    run_stages(groups)
+
+
+def scatter_call(sizes, arrays, collective, total=None, total_at=None):
+    devices = math.prod(sizes)
+    count = len(arrays)
+    shapes = [(array.shape[0] // devices, array.shape[1]) for array in arrays]
+    plan = scatter_plan(shapes)
+    slots = sum(size - 1 for size in sizes)
+    vmem = pl.BlockSpec(memory_space=pltpu.VMEM)
+    operands = [array.reshape(sizes + shape) for array, shape in zip(arrays, shapes)]
+    in_specs, out_specs = [pl.BlockSpec(memory_space=pl.ANY)] * count, [vmem] * count
+    out_shape = [jax.ShapeDtypeStruct(shape, f32) for shape in shapes]
+    parts = sum(map(len, plan))
+    scratch = [
+        pltpu.SemaphoreType.DMA((parts, slots)),
+        pltpu.SemaphoreType.DMA((parts, slots)),
+        pltpu.SemaphoreType.DMA((parts,)),
+    ] + scatter_buffers(sizes, plan, shapes)
+    if total is not None:
+        operands.append(total)
+        in_specs, out_specs = in_specs + [vmem], out_specs + [vmem]
+        out_shape.append(jax.ShapeDtypeStruct(total.shape, f32))
+        scratch += [pltpu.VMEM((sizes[axis],) + total.shape, f32) for axis in (3, 2, 1, 0)]
+        scratch += [pltpu.SemaphoreType.DMA((slots,))] * 2
+    return pl.pallas_call(
+        lambda *refs: scatter_kernel(sizes, plan, count, total_at, *refs),
+        in_specs=in_specs,
+        out_specs=out_specs,
+        out_shape=out_shape,
+        scratch_shapes=scratch,
+        compiler_params=pltpu.CompilerParams(
+            collective_id=collective, has_side_effects=True, vmem_limit_bytes=VMEM_LIMIT
+        ),
+        name="sum_gradients",
+    )(*operands)
+
+
 def layer_norm(values, norm_gain, norm_offset):
     middle = values - jnp.mean(values, axis=-1, keepdims=True)
     spread = jnp.mean(middle * middle, axis=-1, keepdims=True)
@@ -321,6 +704,7 @@
 
 
 def shards(
+    sizes,
     atoms,
     positions,
     segment,
@@ -342,16 +726,18 @@
     cotangent,
 ):
     axes = ("grp", "dev")
-    gather = lambda array, axis: lax.all_gather(array, axes, axis=axis, tiled=True)
-    w_time = gather(time_weight, 1)
-    gain_one, shift_one = gather(norm1_gain, 0).astype(f32), gather(norm1_bias, 0).astype(f32)
-    w_qkv = gather(qkv_weight, 0)
-    w_out = gather(out_weight, 0)
-    gain_two, shift_two = gather(norm2_gain, 0).astype(f32), gather(norm2_bias, 0).astype(f32)
-    w_in = gather(ffn_in, 0)
-    bias_in = gather(ffn_in_bias, 0).astype(f32)
-    w_back = gather(ffn_out, 0)
-    bias_back = gather(ffn_out_bias, 0).astype(f32)
+    own_rows, own_hidden = norm1_gain.shape[0], ffn_in_bias.shape[0]
+    vectors = jnp.stack(
+        [jnp.pad(v, (0, 128 - v.shape[0])) for v in (norm1_gain, norm1_bias, norm2_gain, norm2_bias, ffn_out_bias, ffn_in_bias)]
+        + [jnp.zeros((128,), bf16)] * 2
+    )
+    small = jnp.concatenate([time_weight.T, vectors], axis=0)
+    small, w_qkv, w_out, w_in, w_back = gather_call(sizes, (small, qkv_weight, out_weight, ffn_in, ffn_out), 1)
+    w_qkv, w_out, w_in, w_back = (full.reshape(-1, full.shape[2]) for full in (w_qkv, w_out, w_in, w_back))
+    w_time_t = small[:, :own_rows].reshape(-1, TFREQ)
+    vectors = small[:, own_rows:].astype(f32).transpose(1, 0, 2)
+    gain_one, shift_one, gain_two, shift_two, bias_back = (vectors[at, :, :own_rows].reshape(-1) for at in range(5))
+    bias_in = vectors[5, :, :own_hidden].reshape(-1)
 
     places = jnp.concatenate([positions, segment.astype(f32)[None]], axis=0)
     places_all = jnp.concatenate(of_block(places), axis=1)
@@ -368,7 +754,7 @@
     tables = spread_tables()
 
     features = time_features(item_time).astype(bf16)
-    stream_zero = atoms.astype(f32) + dot(features, w_time)
+    stream_zero = atoms.astype(f32) + times_transposed(features, w_time_t)
     normed = layer_norm(stream_zero, gain_one, shift_one).astype(bf16)
     packed_t = lax.dot_general(w_qkv, normed, (((0,), (1,)), ((), ())), preferred_element_type=f32).astype(bf16)
     q_t = packed_t[:D]
@@ -384,19 +770,19 @@
 
     grad_output = cotangent.astype(f32)
     grad_branch = cotangent
-    grad_back = outer_sum(hidden_act, grad_branch)
+    grad_back = outer_sum(hidden_act, grad_branch).astype(bf16)
     grad_bias_back = jnp.sum(grad_output, axis=0)
     grad_act = times_transposed(grad_branch, w_back)
     _, gelu_pull = jax.vjp(lambda pre: jax.nn.gelu(pre, approximate=False), hidden_pre)
     grad_pre = gelu_pull(grad_act)[0].astype(bf16)
-    grad_in = outer_sum(second, grad_pre)
+    grad_in = outer_sum(second, grad_pre).astype(bf16)
     grad_bias_in = jnp.sum(grad_pre.astype(f32), axis=0)
     grad_second = times_transposed(grad_pre, w_in)
     _, norm_two_pull = jax.vjp(layer_norm, stream_one, gain_two, shift_two)
     grad_stream_part, grad_gain_two, grad_shift_two = norm_two_pull(grad_second)
     grad_stream_one = grad_output + grad_stream_part
     grad_attn = grad_stream_one.astype(bf16)
-    grad_out_weight = dot(mixed_t, grad_attn)
+    grad_out_weight = dot(mixed_t, grad_attn).astype(bf16)
     grad_mixed_t = times_transposed(w_out, grad_attn).astype(bf16)
 
     gs, grad_query_t, grad_key_t, grad_value_t = backward_call(q_t, grad_mixed_t, k_t, v_t, prob, tables)
@@ -409,19 +795,33 @@
     far = part[2] + from_partner(part[3].astype(bf16), 1).astype(f32)
     own = own + from_partner(far.astype(bf16), 2).astype(f32)
     grad_packed_t = jnp.concatenate([grad_query_t, own.astype(bf16)], axis=0)
-    grad_qkv = lax.dot_general(normed, grad_packed_t, (((0,), (1,)), ((), ())), preferred_element_type=f32)
+    grad_qkv = lax.dot_general(normed, grad_packed_t, (((0,), (1,)), ((), ())), preferred_element_type=f32).astype(bf16)
     grad_normed = lax.dot_general(grad_packed_t, w_qkv, (((0,), (1,)), ((), ())), preferred_element_type=f32)
     _, norm_one_pull = jax.vjp(layer_norm, stream_zero, gain_one, shift_one)
     grad_zero_part, grad_gain_one, grad_shift_one = norm_one_pull(grad_normed)
     grad_input = grad_stream_one + grad_zero_part
-    grad_time = outer_sum(features, grad_input.astype(bf16))
-
-    scatter = lambda array, axis: lax.psum_scatter(array, axes, scatter_dimension=axis, tiled=True)
-    sums = lax.psum(sums, axes)
+    grad_time_t = outer_sum(grad_input.astype(bf16), features).astype(bf16)
+
+    vectors = jnp.stack([grad_gain_one, grad_shift_one, grad_gain_two, grad_shift_two, grad_bias_back], axis=1)
+    vectors = jnp.concatenate([vectors, grad_bias_in.reshape(D, -1)], axis=1)
+    vectors = jnp.pad(vectors, ((0, 0), (0, 128 - vectors.shape[1]))).astype(bf16)
+    grad_small = jnp.concatenate([grad_time_t, vectors], axis=1)
+    arrays = (grad_back, grad_in, grad_out_weight, grad_qkv, grad_small)
+    sums = jnp.concatenate(
+        [sums[:HEADS], sums[HEADS : 2 * HEADS] + sums[2 * HEADS : 3 * HEADS], sums[3 * HEADS : 4 * HEADS] + sums[4 * HEADS :]]
+    )
+    if own_rows % 8 == 0:
+        grad_back, grad_in, grad_out_weight, grad_qkv, grad_small, sums = scatter_call(
+            sizes, arrays, 2, total=sums, total_at=0
+        )
+    else:
+        sums = lax.psum(sums, axes)
+        grad_back, grad_in, grad_out_weight, grad_qkv, grad_small = (
+            lax.psum_scatter(array.astype(f32), axes, scatter_dimension=0, tiled=True) for array in arrays
+        )
+    vectors = grad_small[:, TFREQ:]
     weight_t = pair_weight.astype(f32).T
-    low = sums[:HEADS]
-    once = sums[HEADS : 2 * HEADS] + sums[2 * HEADS : 3 * HEADS]
-    twice = sums[3 * HEADS : 4 * HEADS] + sums[4 * HEADS :]
+    low, once, twice = sums[:HEADS], sums[HEADS : 2 * HEADS], sums[2 * HEADS :]
     zeroth, first, square = (jnp.sum(weight_t * part_sum, axis=0) for part_sum in (low, once, twice))
     mean = kernel_mean - center
     grad_mean = (first - mean * zeroth) / (kernel_width * kernel_width)
@@ -431,17 +831,17 @@
     return (
         output,
         grad_input,
-        scatter(grad_time, 1),
-        scatter(grad_gain_one, 0),
-        scatter(grad_shift_one, 0),
-        scatter(grad_qkv, 0),
-        scatter(grad_out_weight, 0),
-        scatter(grad_gain_two, 0),
-        scatter(grad_shift_two, 0),
-        scatter(grad_in, 0),
-        scatter(grad_bias_in, 0),
-        scatter(grad_back, 0),
-        scatter(grad_bias_back, 0),
+        grad_small[:, :TFREQ].T,
+        vectors[:, 0],
+        vectors[:, 1],
+        grad_qkv,
+        grad_out_weight,
+        vectors[:, 2],
+        vectors[:, 3],
+        grad_in,
+        vectors[:, 5 : 5 + own_hidden // own_rows].reshape(-1),
+        grad_back,
+        vectors[:, 4],
         low.T,
         grad_mean,
         grad_width,
@@ -488,4 +888,4 @@
         P(),
         P(),
     )
-    return jax.shard_map(shards, mesh=mesh, in_specs=in_specs, out_specs=out_specs, check_vma=False)
+    return jax.shard_map(partial(shards, grid_of_mesh(mesh)), mesh=mesh, in_specs=in_specs, out_specs=out_specs, check_vma=False)

time: 1150 us -> 549 us (0.48)
  waiting for transfers between devices: 671 us -> 30.9 us
  Pallas kernels: 227 us -> 417 us
  blocking collectives: 126 us -> 0 us
  between operations: 14.8 us -> 1.3 us
  matrix products: 53 us -> 39.7 us
    reduce_scatter x4 -> x0, waiting for transfers between devices: 513 us -> none  [shards(): lax.psum_scatter(array, axes, scatter_dimension=axis, tiled=True)]
    pallas_call x0 -> x2, Pallas kernels: none -> 190 us  [the longest x1 96.6 us: scatter_call(): pl.pallas_call(lambda *refs: scatter_kernel(sizes, plan, count, total_at,...]
    unnamed x2 -> x0, blocking collectives: 82.7 us -> none
    psum x1 -> x0, waiting for transfers between devices: 81 us -> none  [shards(): sums = lax.psum(sums, axes)]
    unnamed x11 -> x0, waiting for transfers between devices: 56.7 us -> none
    all_gather x1 -> x0, blocking collectives: 42.8 us -> none  [shards(): lax.all_gather(array, axes, axis=axis, tiled=True)]
  transfers between devices with their start and end apart: 19 -> 9, of which waited for: 8 -> 2; matrix products, arithmetic and copies ran while one was open for 7% -> 8% of each run, Pallas kernels for 15% -> 27%
where the time goes in v2:
time: 549 us; the launch traced here: 547 us
  Pallas kernels  417 us (76%)
  matrix products  39.7 us (7%)
  local copies, waits for them, and re-layouts  33.1 us (6%)
  waiting for transfers between devices  30.9 us (6%)
  other arithmetic  19 us (3%)
    pallas_call x1, Pallas kernels, scatter_call(): pl.pallas_call(lambda *refs: scatter_kernel(sizes, plan, count, total_at,...  96.6 us
    pallas_call x1, Pallas kernels, gather_call(): pl.pallas_call(lambda *refs: gather_kernel(sizes, plan, count, *refs), in...  93.1 us
    pallas_call x1, Pallas kernels, forward_call(): pl.pallas_call(forward_kernel, grid=(GROUPS, blocks), in_specs=[pl.BlockS...  71 us
    pallas_call x1, Pallas kernels, backward_call(): pl.pallas_call(backward_kernel, grid=(GROUPS, blocks), in_specs=[pl.Block...  57 us
    pallas_call x1, Pallas kernels, pair_call(): pl.pallas_call(pair_kernel, grid=(steps,), in_specs=[pl.BlockSpec((PAIR_R...  53.9 us
    pallas_call x1, Pallas kernels, pair_grad_call(): pl.pallas_call(pair_grad_kernel, grid=(steps,), in_specs=[pl.BlockSpec((G...  45.9 us
    ppermute x9, waiting for transfers between devices, from_partner(): return lax.ppermute(block, 'dev', [(at, at ^ bit) for at in range(count)])  30.9 us
    dot_general x3, matrix products, dot(): return jnp.dot(left, right, preferred_element_type=f32)  15 us
  transfers between devices with their start and end apart: 9, of which 2 were waited for; matrix products, arithmetic and copies ran while one was open for 8% of the time, Pallas kernels for 27%

profile of v2, /device:TPU:0, one launch (start us, length us, event | category | flops | bytes accessed | tf_op | source)
XLA Modules:
  0.0 546.8 jit_solution(15474484053768804110)
XLA Ops:
  1.3 1.3 pad_maximum_fusion.11
  3.1 2.5 collective-permute-start.4
  7.6 1.9 concatenate.37.refs_0_
  9.5 93.1 %gather_weights.1 = (bf16[4,2,2,2,32,128]{5,4,3,2,1,0:T(8,128)(2,1)}, bf16[4,2,2,2,24,2304]{5,4,3,2,1,0:T(8,128)(2,1)}, bf16[4,2,2,2,24,768]{5,4,3,2,1,0:T(8,128...) custom-call(bf16[32,128]{1,0:T(8,128)(2,1)} %concatenate.37.refs_0_, ...), custom_call_target="tpu_custom_call" | custom-call | tf_op jit(solution)/shard_map/gather_weights/pallas_call | solution.py:433
  102.6 0.8 slice.150
  103.4 0.9 slice.149
  106.2 1.4 fusion.46
  108.4 3.3 convolution_convert_fusion.3
  112.6 1.7 fusion.15.spread
  115.1 0.9 fusion.12.head_t
  116.0 15.8 %collective-permute-done.1 = bf16[1536,256]{1,0:T(8,128)(2,1)S(1)} collective-permute-done((bf16[1536,256]{1,0:T(8,128)(2,1)S(1)}, bf16[1536,256]{1,0:T(8,128)(2,1)S(1)}, u32[]{:S(2)}, u32[]{:S(2)}) %collective-permute-start.1) | collective-permute-done | bytes 786464 | tf_op jit(solution)/shard_map/ppermute | solution.py:688
  131.8 1.6 fusion.11.head
  134.8 1.3 slice.162
  137.6 0.8 copy.48.segs_i
  139.2 1.4 add.147
  140.6 1.4 add.151
  141.9 0.8 mul.239
  142.7 0.8 add.144
  143.6 1.3 pad_maximum_fusion.10.segs_j
  144.9 1.3 pad_maximum_fusion.9
  146.2 53.9 %pair_forward.1 = (f32[256,1024]{1,0:T(8,128)}, bf16[32,128,8192]{2,1,0:T(8,128)(2,1)}, f32[4,2048,1024]{2,1,0:T(8,128)}) custom-call(f32[256,3]{1,0:T(8,128)} %copy.47.places_i, f32[256,1]{1,0:T(8,128)} %copy.48.segs_i, f32[3,1024]{1,0:T(4,128)} %bitcast.72, f32[1,1024]{1,0:T(1,128)} %pad_maximum_fusion.10.segs_j, f32[3,128,128]{2,1,0:T(8,128)} %pad_maximum_fusion.4.coef, ...), custom_call_target="tpu_custom_call" | custom-call | tf_op jit(solution)/shard_map/pair_forward/pallas_call | solution.py:72
  200.1 1.5 pad_maximum_fusion
  201.6 1.9 fusion.43
  203.5 71.0 %attention_forward.1 = (bf16[768,256]{1,0:T(8,128)(2,1)}, bf16[4,2048,1024]{2,1,0:T(8,128)(2,1)}) custom-call(bf16[768,256]{1,0:T(8,128)(2,1)} %slice.153.q_ref, bf16[768,1024]{1,0:T(8,128)(2,1)} %get-tuple-element.79.k_ref, bf16[768,1024]{1,0:T(8,128)(2,1)} %get-tuple-element.78.v_ref, f32[4,2048,1024]{2,1,0:T(8,128)} %get-tuple-element.38.bias_ref, ...), custom_call_target="tpu_custom_call" | custom-call | tf_op jit(solution)/shard_map/attention_forward/pallas_call | solution.py:142
  274.5 1.7 fusion.47
  276.5 11.2 %multiply_convert_fusion = (bf16[256,3072]{1,0:T(8,128)(2,1)}, f32[256,3072]{1,0:T(8,128)S(1)}, f32[256,3072]{1,0:T(8,128)S(1)}) fusion(f32[3072]{0:T(1024)S(1)} %copy-done.23, bf16[768,3072]{1,0:T(8,128)(2,1)} %bitcast.86, f32[256,768]{1,0:T(8,128)S(1)} %get-tuple-element.98, f32[768]{0:T(1024)S(1)} %add.144, f32[768]{0:T(1024)S(1)} %mul.239, ...), kind=kOutput, calls=%fused_computation.10 | convolution fusion | flops 1260847104 | bytes 13389824 | tf_op jit(solution)/shard_map/dot_general | solution.py:37
  287.8 2.2 fusion.48
  290.0 1.6 multiply_reduce_fusion
  292.8 2.5 convolution_convert_fusion.5.go_ref
  295.3 57.0 %attention_backward.1 = (bf16[4,2048,1024]{2,1,0:T(8,128)(2,1)}, bf16[768,256]{1,0:T(8,128)(2,1)}, f32[768,1024]{1,0:T(8,128)}, f32[768,1024]{1,0:T(8,128)}) custom-call(bf16[768,256]{1,0:T(8,128)(2,1)} %slice.153.q_ref, bf16[768,256]{1,0:T(8,128)(2,1)} %convolution_convert_fusion.5.go_ref, bf16[768,1024]{1,0:T(8,128)(2,1)} %get-tuple-element.79.k_ref, ...), custom_call_target="tpu_custom_call" | custom-call | tf_op jit(solution)/shard_map/attention_backward/pallas_call | solution.py:212
  352.3 45.9 %pair_gradient.1 = f32[160,128]{1,0:T(8,128)} custom-call(bf16[4,2048,1024]{2,1,0:T(8,128)(2,1)} %get-tuple-element.47.gs_ref, f32[256,1024]{1,0:T(8,128)} %get-tuple-element.48.dist_ref, bf16[32,128,8192]{2,1,0:T(8,128)(2,1)} %get-tuple-element.49.phi_ref), custom_call_target="tpu_custom_call" | custom-call | tf_op jit(solution)/shard_map/pair_gradient/pallas_call | solution.py:275
  399.3 1.7 copy-done.2
  403.1 3.6 convolution_convert_fusion.2
  406.7 3.7 convolution_convert_fusion.1
  411.4 1.5 convolution_convert_fusion.4
  412.9 2.2 fusion.10
  415.2 15.1 %collective-permute-done.8 = bf16[1536,256]{1,0:T(8,128)(2,1)S(1)} collective-permute-done((bf16[1536,256]{1,0:T(8,128)(2,1)S(1)}, bf16[1536,256]{1,0:T(8,128)(2,1)S(1)}, u32[]{:S(2)}, u32[]{:S(2)}) %collective-permute-start.8) | collective-permute-done | bytes 786464 | tf_op jit(solution)/shard_map/ppermute | solution.py:688
  430.7 1.3 multiply_reduce_fusion.1
  432.0 3.1 convolution_convert_fusion
  436.4 0.9 copy.50
  437.3 96.6 %sum_gradients.1 = (f32[96,768]{1,0:T(8,128)}, f32[24,3072]{1,0:T(8,128)}, f32[24,768]{1,0:T(8,128)}, f32[24,2304]{1,0:T(8,128)}, f32[24,256]{1,0:T(8,128)}, /*index=5*/f32[96,128]{1,0:T(8,128)}) custom-call(bf16[4,2,2,2,96,768]{5,4,3,2,1,0:T(8,128)(2,1)} %bitcast.62, bf16[4,2,2,2,24,3072]{5,4,3,2,1,0:T(8,128)(2,1)} %bitcast.63, ...), custom_call_target="tpu_custom_call" | custom-call | tf_op jit(solution)/shard_map/sum_gradients/pallas_call | solution.py:660
  533.9 1.7 slice_reduce_fusion
  536.4 1.3 slice_bitcast_fusion.1
  538.4 1.4 fusion.24
  540.2 1.6 copy.59
  541.9 1.5 copy.60
  543.4 1.7 copy.61
  545.1 1.7 copy.62
  (160 shorter events, 20.1 us)
Async XLA Ops:
  1.3 104.4 %copy-start.17 = (f32[256]{0:T(256)}, f32[256]{0:T(256)S(1)}, u32[]{:S(2)}) copy-start(f32[256]{0:T(256)S(1)} %convert_element_type.108) | copy-start | bytes 3076
  2.6 140.9 %collective-permute-start.3 = (f32[4,256]{1,0:T(4,128)}, f32[4,256]{1,0:T(4,128)}, u32[]{:S(2)}, u32[]{:S(2)}) collective-permute-start(f32[4,256]{1,0:T(4,128)} %pad_maximum_fusion.11), channel_id=1, source_target_pairs={{0,1},{1,0},{2,3},{3,2},{4,5},{5,4},{6,7},{7,6},{8,9},{9,8},{10,11... | collective-permute-start | bytes 12296 | tf_op jit(solution)/shard_map/ppermute | solution.py:688
  3.1 131.2 %collective-permute-start.4 = (f32[4,256]{1,0:T(4,128)}, f32[4,256]{1,0:T(4,128)}, u32[]{:S(2)}, u32[]{:S(2)}) collective-permute-start(f32[4,256]{1,0:T(4,128)} %pad_maximum_fusion.11), channel_id=1, source_target_pairs={{0,2},{1,3},{2,0},{3,1},{4,6},{5,7},{6,4},{7,5},{8,10},{9,11},{10,... | collective-permute-start | bytes 12296 | tf_op jit(solution)/shard_map/ppermute | solution.py:688
  105.0 1.2 copy-start.9
  106.2 1.7 copy-start.11
  106.2 1.7 copy-start.13
  107.6 0.5 copy-start.19
  107.8 0.5 copy-start.25
  107.9 0.5 copy-start.21
  108.4 23.4 %copy-start.30 = (f32[128]{0:T(128)S(1)}, f32[128]{0:T(128)}, u32[]{:S(2)}) copy-start(f32[128]{0:T(128)} %param.36) | copy-start | bytes 1540
  111.7 21.8 %copy-start.28 = (f32[128]{0:T(128)S(1)}, f32[128]{0:T(128)}, u32[]{:S(2)}) copy-start(f32[128]{0:T(128)} %param.35) | copy-start | bytes 1540
  111.7 23.1 %copy-start.15 = (f32[3,256]{1,0:T(4,128)S(1)}, f32[3,256]{1,0:T(4,128)}, u32[]{:S(2)}) copy-start(f32[3,256]{1,0:T(4,128)} %param.20) | copy-start | bytes 9220
  111.7 23.1 %copy-start.18 = (f32[256]{0:T(256)S(1)}, f32[256]{0:T(256)}, u32[]{:S(2)}) copy-start(f32[256]{0:T(256)} %copy-done.17) | copy-start | bytes 3076
  111.7 25.2 %copy-start = (bf16[256,768]{1,0:T(8,128)(2,1)S(1)}, bf16[256,768]{1,0:T(8,128)(2,1)}, u32[]{:S(2)}) copy-start(bf16[256,768]{1,0:T(8,128)(2,1)} %param.37) | copy-start | bytes 1179652
  111.8 20.0 %collective-permute-start.1 = (bf16[1536,256]{1,0:T(8,128)(2,1)S(1)}, bf16[1536,256]{1,0:T(8,128)(2,1)S(1)}, u32[]{:S(2)}, u32[]{:S(2)}) collective-permute-start(bf16[1536,256]{1,0:T(8,128)(2,1)S(1)} %slice.154), channel_id=1, source_target_pairs={{0,2},{1,3},{2,0},{3,1},{4,6},{5,7},{6,4},{7,5},{8,10},{9,11},{10,... | collective-permute-start | bytes 2359304 | tf_op jit(solution)/shard_map/ppermute | solution.py:688
  112.4 87.7 %collective-permute-start = (bf16[1536,256]{1,0:T(8,128)(2,1)S(1)}, bf16[1536,256]{1,0:T(8,128)(2,1)S(1)}, u32[]{:S(2)}, u32[]{:S(2)}) collective-permute-start(bf16[1536,256]{1,0:T(8,128)(2,1)S(1)} %slice.154), channel_id=1, source_target_pairs={{0,1},{1,0},{2,3},{3,2},{4,5},{5,4},{6,7},{7,6},{8,9},{9,8},{10,11... | collective-permute-start | bytes 2359304 | tf_op jit(solution)/shard_map/ppermute | solution.py:688
  131.7 68.4 %collective-permute-start.2 = (bf16[1536,256]{1,0:T(8,128)(2,1)S(1)}, bf16[1536,256]{1,0:T(8,128)(2,1)}, u32[]{:S(2)}, u32[]{:S(2)}) collective-permute-start(bf16[1536,256]{1,0:T(8,128)(2,1)S(1)} %collective-permute-done.1), channel_id=1, source_target_pairs={{0,1},{1,0},{2,3},{3,2},{4,5},{5,4},{6,7},{7,6},{8,9},{9,8},{10,11... | collective-permute-start | bytes 2359304 | tf_op jit(solution)/shard_map/ppermute | solution.py:688
  134.3 9.3 %collective-permute-start.5 = (f32[4,256]{1,0:T(4,128)}, f32[4,256]{1,0:T(4,128)}, u32[]{:S(2)}, u32[]{:S(2)}) collective-permute-start(f32[4,256]{1,0:T(4,128)} %collective-permute-done.4), channel_id=1, source_target_pairs={{0,1},{1,0},{2,3},{3,2},{4,5},{5,4},{6,7},{7,6},{8,9},{9,8},{10,11... | collective-permute-start | bytes 12296 | tf_op jit(solution)/shard_map/ppermute | solution.py:688
  203.5 71.0 %copy-start.8 = (bf16[4,2,2,2,24,768]{5,4,3,2,1,0:T(8,128)(2,1)S(1)}, bf16[4,2,2,2,24,768]{5,4,3,2,1,0:T(8,128)(2,1)}, u32[]{:S(2)}) copy-start(bf16[4,2,2,2,24,768]{5,4,3,2,1,0:T(8,128)(2,1)} %get-tuple-element.40) | copy-start | bytes 3538948
  274.5 2.0 copy-start.23
  274.5 13.3 %slice-start = ((s8[4718592]{0:T(1024)(128)(4,1)}), s8[4194304]{0:T(1024)(128)(4,1)S(1)}, s32[]{:S(2)}) async-start(s8[4718592]{0:T(1024)(128)(4,1)} %bitcast.80), calls=%async_computation | async-start | bytes 8388608
  274.5 15.5 %slice-start.4 = ((s8[4718592]{0:T(1024)(128)(4,1)}), s8[4194304]{0:T(1024)(128)(4,1)S(1)}, s32[]{:S(2)}) async-start(s8[4718592]{0:T(1024)(128)(4,1)} %bitcast.87), calls=%async_computation.4 | async-start | bytes 8388608
  276.5 11.3 %slice-start.1 = ((s8[4718592]{0:T(1024)(128)(4,1)}), s8[524288]{0:T(1024)(128)(4,1)S(1)}, s32[]{:S(2)}) async-start(s8[4718592]{0:T(1024)(128)(4,1)} %bitcast.80), calls=%async_computation.1 | async-start | bytes 1048576
  276.5 13.5 %slice-start.5 = ((s8[4718592]{0:T(1024)(128)(4,1)}), s8[524288]{0:T(1024)(128)(4,1)S(1)}, s32[]{:S(2)}) async-start(s8[4718592]{0:T(1024)(128)(4,1)} %bitcast.87), calls=%async_computation.5 | async-start | bytes 1048576
  290.0 1.6 copy-start.5
  352.3 46.7 %copy-start.3 = (f32[768,1024]{1,0:T(8,128)S(1)}, f32[768,1024]{1,0:T(8,128)}, u32[]{:S(2)}) copy-start(f32[768,1024]{1,0:T(8,128)} %get-tuple-element.45) | copy-start | bytes 9437188
  399.0 1.9 copy-start.2
  401.7 1.4 copy-start.1
  401.8 13.4 %collective-permute-start.6 = (bf16[1536,256]{1,0:T(8,128)(2,1)S(1)}, bf16[1536,256]{1,0:T(8,128)(2,1)S(1)}, u32[]{:S(2)}, u32[]{:S(2)}) collective-permute-start(bf16[1536,256]{1,0:T(8,128)(2,1)S(1)} %get-tuple-element.76), channel_id=1, source_target_pairs={{0,1},{1,0},{2,3},{3,2},{4,5},{5,4},{6,7},{7,6},{8,9},{9,8},{10,11... | collective-permute-start | bytes 2359304 | tf_op jit(solution)/shard_map/ppermute | solution.py:688
  401.9 8.5 %collective-permute-start.7 = (bf16[1536,256]{1,0:T(8,128)(2,1)S(1)}, bf16[1536,256]{1,0:T(8,128)(2,1)S(1)}, u32[]{:S(2)}, u32[]{:S(2)}) collective-permute-start(bf16[1536,256]{1,0:T(8,128)(2,1)S(1)} %get-tuple-element.77), channel_id=1, source_target_pairs={{0,1},{1,0},{2,3},{3,2},{4,5},{5,4},{6,7},{7,6},{8,9},{9,8},{10,11... | collective-permute-start | bytes 2359304 | tf_op jit(solution)/shard_map/ppermute | solution.py:688
  403.1 3.6 copy-start.6
  403.1 9.8 %slice-start.2 = ((s8[4718592]{0:T(1024)(128)(4,1)}), s8[4194304]{0:T(1024)(128)(4,1)S(1)}, s32[]{:S(2)}) async-start(s8[4718592]{0:T(1024)(128)(4,1)} %bitcast.83), calls=%async_computation.2 | async-start | bytes 8388608
  406.7 6.3 %slice-start.3 = ((s8[4718592]{0:T(1024)(128)(4,1)}), s8[524288]{0:T(1024)(128)(4,1)S(1)}, s32[]{:S(2)}) async-start(s8[4718592]{0:T(1024)(128)(4,1)} %bitcast.83), calls=%async_computation.3 | async-start | bytes 1048576
  410.4 1.0 copy-start.7
  410.4 2.5 copy-start.27
  410.7 19.5 %collective-permute-start.8 = (bf16[1536,256]{1,0:T(8,128)(2,1)S(1)}, bf16[1536,256]{1,0:T(8,128)(2,1)S(1)}, u32[]{:S(2)}, u32[]{:S(2)}) collective-permute-start(bf16[1536,256]{1,0:T(8,128)(2,1)S(1)} %fusion.6), channel_id=1, source_target_pairs={{0,2},{1,3},{2,0},{3,1},{4,6},{5,7},{6,4},{7,5},{8,10},{9,11},{10,... | collective-permute-start | bytes 2359304 | tf_op jit(solution)/shard_map/ppermute | solution.py:688
  412.9 17.7 %copy-start.32 = (bf16[4,2,2,2,24,2304]{5,4,3,2,1,0:T(8,128)(2,1)S(1)}, bf16[4,2,2,2,24,2304]{5,4,3,2,1,0:T(8,128)(2,1)}, u32[]{:S(2)}) copy-start(bf16[4,2,2,2,24,2304]{5,4,3,2,1,0:T(8,128)(2,1)} %get-tuple-element.37) | copy-start | bytes 10616836
  415.1 15.5 %copy-start.10 = (bf16[768,256]{1,0:T(8,128)(2,1)S(1)}, bf16[768,256]{1,0:T(8,128)(2,1)}, u32[]{:S(2)}) copy-start(bf16[768,256]{1,0:T(8,128)(2,1)} %get-tuple-element.44) | copy-start | bytes 1179652
  415.1 15.5 %copy-start.20 = (f32[256]{0:T(256)S(1)}, f32[256]{0:T(256)}, u32[]{:S(2)}) copy-start(f32[256]{0:T(256)} %copy-done.19) | copy-start | bytes 3076
  415.1 15.5 %copy-start.22 = (f32[256]{0:T(256)S(1)}, f32[256]{0:T(256)}, u32[]{:S(2)}) copy-start(f32[256]{0:T(256)} %copy-done.21) | copy-start | bytes 3076
  432.0 3.2 copy-start.26
  435.2 0.8 copy-start.12
  435.2 0.8 copy-start.14
  435.2 1.0 copy-start.24
  436.0 98.0 %copy-start.4 = (f32[256,768]{1,0:T(8,128)}, f32[256,768]{1,0:T(8,128)S(1)}, u32[]{:S(2)}) copy-start(f32[256,768]{1,0:T(8,128)S(1)} %add_add_fusion.2) | copy-start | bytes 2359300
  437.3 101.0 %copy-start.16 = (bf16[128,32]{0,1:T(8,128)(2,1)S(1)}, bf16[128,32]{0,1:T(8,128)(2,1)}, u32[]{:S(2)}) copy-start(bf16[128,32]{0,1:T(8,128)(2,1)} %param.34) | copy-start | bytes 24580
  437.3 102.4 %copy-start.29 = (f32[128]{0:T(128)S(1)}, f32[128]{0:T(128)}, u32[]{:S(2)}) copy-start(f32[128]{0:T(128)} %param.35) | copy-start | bytes 1540
  437.3 102.4 %copy-start.31 = (f32[128]{0:T(128)S(1)}, f32[128]{0:T(128)}, u32[]{:S(2)}) copy-start(f32[128]{0:T(128)} %param.36) | copy-start | bytes 1540
